TPU v7x, 256 devices: a whole 4x4x8 slice. The times are simulated.
256 devices in a mesh: rad: 4 (over x_hi, core), lat: 64 (over x_lo, z, y).
Axes of the slice: x: 4 (x_hi: 2, x_lo: 2; x = x_hi * 2 + x_lo), y: 4, z: 8, core: 2. Of those that a mesh axis runs over, the one named last changes fastest.
Arguments:
- velocity: bfloat16 [3, 128, 768, 1536], P(None, 'rad', 'lat'), may hold values from -6 to 6
- density: float32 [128], P('rad'), may hold values from 0.3 to 3
- offsets: int32 [4], replicated, may hold values from -3 to 3, as said below
- radial_weights: float32 [2, 4, 128], P(None, None, 'rad'), may hold values from -3 to 3
- angular_scale: float32 [128], P('rad'), may hold values from 9.536743e-07 to 3.8146973e-06
- order_table: int32 [512], replicated, may hold values from 0 to 511, as said below
- eigenfunctions: float32 [512, 32, 128], P(None, None, 'rad'), may hold values from -0.5 to 0.5
Outputs:
- coeffs: float32 [512, 2, 32, 512], P('lat', None, 'rad')
Inputs may be any that keep to these rules, and one draw needn't show every extreme that they name: 4 distinct offsets; minus 3 and 3 are among them. `order_table`: a permutation of the orders; for every k, slots 2k and 2k + 1 hold orders m and 511 - m.
All inputs are finite; a program needn't handle non-finite values.
Results may differ from a plain program's by a relative error of at most 0.0003.
Values sent between devices are 32-bit elements; how exact they have to be, the bound alone decides.
No kernel may reach another device: no remote copies, remote signals or barrier semaphores. Data moves between devices by JAX's collectives and lax.ppermute only.
A program may use at most 128 MiB of HBM per device.

v0:
```python
import jax
import jax.numpy as jnp
from jax import lax
from jax.sharding import PartitionSpec as P

TAPS = 4
HALO = 3


def extended(value, sides, width):
    for axis, dim in sides:
        size, length = (lax.axis_size(axis), value.shape[dim])
        up = [(i, (i + 1) % size) for i in range(size - 1)]
        down = [(j, i) for i, j in up]
        last = lax.slice_in_dim(value, length - width, length, axis=dim)
        initial = lax.slice_in_dim(value, 0, width, axis=dim)
        before = lax.ppermute(last, axis, up)
        after = lax.ppermute(initial, axis, down)
        value = jnp.concatenate([before, value, after], axis=dim)
    return value


def split_up(value, dim, size):
    dims = value.shape
    pieces = value.reshape(*dims[:dim], size, dims[dim] // size, *dims[dim + 1 :])
    return jnp.moveaxis(pieces, dim, 0)


def in_order(pieces, dim):
    dims = list(pieces.shape[1:])
    dims[dim] *= pieces.shape[0]
    return jnp.moveaxis(pieces, 0, dim).reshape(dims)


def joined_exchange(value, axis, axes, splits, concats):
    sizes = [lax.axis_size(a) for a in axes]
    pieces = split_up(value, splits[0], sizes[0])
    pieces = jnp.moveaxis(split_up(pieces, splits[1] + 1, sizes[1]), 0, 1)
    inside = pieces.shape[2:]
    pieces = pieces.reshape(-1, *inside)
    pieces = lax.all_to_all(pieces, axis, split_axis=0, concat_axis=0, tiled=True)
    pieces = in_order(pieces.reshape(*sizes, *inside), concats[0] + 1)
    return in_order(pieces, concats[1])


def legendre_rows(orders, lat_count, degrees):
    colatitude = jnp.pi * (jnp.arange(lat_count, dtype=jnp.float32) + 0.5) / lat_count
    cosine = jnp.cos(colatitude)
    sine = jnp.sin(colatitude)
    order_float = orders.astype(jnp.float32)
    ladder = jnp.arange(1, degrees, dtype=jnp.float32)
    log_steps = jnp.concatenate(
        [
            jnp.zeros((1,), jnp.float32),
            jnp.cumsum(0.5 * jnp.log((2.0 * ladder + 1.0) / (2.0 * ladder))),
        ]
    )
    log_start = 0.5 * jnp.log(jnp.ones((), jnp.float32) * 0.5) + jnp.take(log_steps, orders)
    log_diagonal = log_start[:, None] + order_float[:, None] * jnp.log(sine)[None, :]

    def advance(state, degree):
        previous, older, exponent = state
        level = degree.astype(jnp.float32)
        upward = jnp.sqrt(
            (4.0 * level * level - 1.0)
            / jnp.maximum(level * level - order_float * order_float, 1.0)
        )
        backward = jnp.sqrt(
            jnp.maximum((level - 1.0) * (level - 1.0) - order_float * order_float, 0.0)
            / jnp.maximum(4.0 * (level - 1.0) * (level - 1.0) - 1.0, 1.0)
        )
        recurred = upward[:, None] * (cosine[None, :] * previous - backward[:, None] * older)
        starting = (degree == orders)[:, None]
        scaled = jnp.where(
            starting,
            jnp.ones_like(recurred),
            jnp.where((degree > orders)[:, None], recurred, jnp.zeros_like(recurred)),
        )
        exponent = jnp.where(starting, log_diagonal, exponent)
        ratio = jnp.maximum(jnp.abs(scaled), 1.0)
        scaled = scaled / ratio
        previous = previous / ratio
        exponent = exponent + jnp.log(ratio)
        return ((scaled, previous, exponent), (scaled, exponent))

    zeros = jnp.zeros((orders.shape[0], lat_count), jnp.float32)
    _, outputs = lax.scan(
        advance, (zeros, zeros, zeros), jnp.arange(degrees, dtype=jnp.int32), unroll=32
    )
    rows = outputs[0] * jnp.exp(outputs[1])
    weight = jnp.sqrt(jnp.pi / lat_count) * sine
    return rows * weight[None, None, :]


def spectral_source(part, rows):
    transformed = jnp.einsum("fijco,loj->fiocl", part, rows, precision=lax.Precision.HIGHEST)
    level = jnp.arange(rows.shape[0], dtype=jnp.float32)
    degree_factor = level * (level + 1.0)
    return transformed[0] - degree_factor * transformed[1]


def fourier_table(lon_count, degrees):
    longitude = jnp.arange(lon_count, dtype=jnp.int32)[:, None]
    wave = jnp.arange(degrees, dtype=jnp.int32)[None, :]
    angle = 2.0 * jnp.pi * (longitude * wave % lon_count).astype(jnp.float32) / lon_count
    scale = 1.0 / jnp.sqrt(jnp.ones((), jnp.float32) * lon_count)
    return jnp.concatenate([jnp.cos(angle), -jnp.sin(angle)], axis=1) * scale


def body(velocity, density, offsets, radial_weights, angular_scale, order_table, eigenfunctions):
    shells = velocity.shape[1]
    lat_local = velocity.shape[2]
    lon_count = velocity.shape[3]
    degrees = order_table.shape[0]
    lat_groups = lax.axis_size("lat")
    rad_groups = lax.axis_size("rad")
    per_device = degrees // lat_groups
    lat_count = lat_local * lat_groups
    flow = velocity.astype(jnp.float32)
    radial, polar, azimuth = (flow[0], flow[1], flow[2])
    rho = density[:, None, None]
    cross = jnp.stack([rho * radial * polar, rho * radial * azimuth])
    padded = extended(cross, (("rad", 1),), HALO)
    radial_term = jnp.zeros_like(radial)
    for tap in range(TAPS):
        shifted = lax.dynamic_slice_in_dim(padded, HALO + offsets[tap], shells, 1)
        radial_term = (
            radial_term
            + radial_weights[0, tap][:, None, None] * shifted[0]
            + radial_weights[1, tap][:, None, None] * shifted[1]
        )
    angular_term = (
        angular_scale[:, None, None]
        * rho
        * (polar * polar + azimuth * azimuth - 2.0 * radial * radial + polar * azimuth)
    )
    fields = jnp.stack([radial_term, angular_term]).reshape(2 * shells * lat_local, lon_count)
    spectrum = jnp.dot(
        fields,
        fourier_table(lon_count, degrees),
        precision=lax.Precision.HIGHEST,
        preferred_element_type=jnp.float32,
    ).reshape(2, shells, lat_local, 2, degrees)
    quarter = per_device // rad_groups
    slot_order = (
        order_table.reshape(lat_groups, rad_groups, quarter).transpose(1, 0, 2).reshape(degrees)
    )
    by_slot = jnp.take(spectrum, slot_order, axis=4)
    gathered = joined_exchange(by_slot, ("rad", "lat"), ("rad", "lat"), (4, 4), (1, 2))
    first_slot = lax.axis_index("lat") * per_device + lax.axis_index("rad") * quarter
    my_orders = lax.dynamic_slice_in_dim(order_table, first_slot, quarter)
    rows = legendre_rows(my_orders, lat_count, degrees)
    source = spectral_source(gathered, rows)
    totals = jnp.einsum(
        "rocl,lnr->ocnl",
        source,
        lax.all_gather(eigenfunctions, "rad", axis=2, tiled=True),
        precision=lax.Precision.HIGHEST,
    )
    return lax.all_to_all(totals, "rad", split_axis=2, concat_axis=0, tiled=True)


def solution(mesh):
    placed = (
        P(None, "rad", "lat", None),
        P("rad"),
        P(),
        P(None, None, "rad"),
        P("rad"),
        P(),
        P(None, None, "rad"),
    )
    return jax.shard_map(
        body, mesh=mesh, in_specs=placed, out_specs=P("lat", None, "rad", None), check_vma=False
    )
```

profile of v0, /device:TPU:1, one launch (start us, length us, event | category | flops | bytes accessed | tf_op | source)
XLA Modules:
  0.0 1060.9 jit_solution(13208825574536134483)
XLA Ops:
  25.5 14.0 %sine_negate_fusion = (f32[1536,512]{0,1:T(8,128)}, f32[1536,512]{0,1:T(8,128)}) fusion(), kind=kLoop, calls=%fused_computation.412 | loop fusion | flops 7864320 | bytes 6291456 | tf_op jit(solution)/shard_map/neg | solution.py:107
  60.5 13.3 %fusion.117 = f32[1,32,12,1536]{3,1,2,0:T(8,128)} fusion(f32[2,38,12,1536]{3,1,2,0:T(8,128)} %pad_maximum_fusion, s32[]{:T(128)S(6)} %add.1080, s32[]{:T(128)S(6)} %select_n.737, s32[]{:T(128)S(6)} %select_n.736, s32[]{:T(128)S(6)} %select_n.735, s32[]{:T(128)S(6)} %select_n.734, f32[32]{0:T(128)S(1)} %get-tuple-element.841, f32[32]{0:T(128)S(1)} %get-tuple-element.842, ...), kind=kLoop, calls=%fused_computation.423 | loop fusion | flops 8847360 | bytes 21234708 | tf_op jit(solution)/shard_map/add | solution.py:128
  73.8 19.2 %fusion.102 = f32[2,32,12,2,512]{4,1,3,2,0:T(8,128)} fusion(f32[2,512,1536,1,1]{2,1,0,4,3:T(8,128)} %bitcast.550, f32[1,32,12,1536]{3,1,2,0:T(8,128)S(1)} %copy-done.2, f32[1,32,12,1536]{3,1,2,0:T(8,128)} %fusion.117), kind=kOutput, calls=%fused_computation.402 | convolution fusion | flops 14496694272 | bytes 14155776 | tf_op jit(solution)/shard_map/dot_general | solution.py:138
  93.1 17.0 %copy.47 = f32[2,32,12,2,512]{1,3,4,2,0:T(2,128)} copy(f32[2,32,12,2,512]{4,1,3,2,0:T(8,128)} %fusion.102) | data formatting | bytes 6291456 | tf_op jit(solution)/shard_map/dot_general | solution.py:138
  110.1 36.0 %gather_fusion.1 = f32[512,2,32,12,2]{2,4,3,1,0:T(2,128)} fusion(f32[2,32,12,2,512]{1,3,4,2,0:T(2,128)} %copy.47, s32[1024]{0:T(1024)S(1)} %pad_clamp_fusion), kind=kCustom, calls=%fused_computation.1 | custom fusion | bytes 6293504 | tf_op jit(solution)/shard_map/jit(_take)/gather | solution.py:148
  146.0 13.9 %copy_select_fusion = f32[2,32,12,2,4,128]{1,5,3,2,0,4:T(8,128)} fusion(f32[2,32,12,2,4,128]{1,3,2,0,5,4:T(2,128)} %bitcast.546, pred[4,128]{1,0:T(4,128)(4,1)S(1)} %copy.41), kind=kLoop, calls=%fused_computation.397 | loop fusion | flops 786432 | bytes 6291968 | tf_op jit(solution)/shard_map/jit(_take)/select_n | solution.py:148
  159.9 11.6 %copy.66 = f32[4,64,2,32,12,2,2]{3,6,5,4,2,1,0:T(2,128)} copy(f32[4,64,2,32,12,2,2]{3,6,1,5,4,2,0:T(2,128)} %bitcast.541) | data formatting | bytes 6291456 | tf_op jit(solution)/shard_map/reshape | solution.py:40
  171.5 15.4 %reshape.1660 = f32[256,1,3072]{2,1,0:T(1,128)} reshape(f32[256,2,12,2,2,32]{5,4,3,2,1,0:T(2,128)} %bitcast.542) | data formatting | bytes 6291456
  186.9 15.5 %all-to-all-start = ((f32[256,1,3072]{2,1,0:T(1,128)}), f32[256,1,3072]{2,1,0:T(1,128)}, u32[]{:S(2)}, u32[]{:S(2)}) async-start(f32[256,1,3072]{2,1,0:T(1,128)} %reshape.1660), calls=%async_computation | async-start | bytes 6291456 | tf_op jit(solution)/shard_map/all_to_all | solution.py:41
  202.5 743.1 %while.23 = (s32[]{:T(128)}, f32[2,768]{1,0:T(2,128)S(1)}, f32[2,768]{1,0:T(2,128)S(1)}, f32[2,768]{1,0:T(2,128)S(1)}, f32[16,32,2,768]{3,2,1,0:T(2,128)}, /*ind...) while((s32[]{:T(128)}, f32[2,768]{1,0:T(2,128)S(1)}, ...), condition=%wide.region_3.4_spmd.clone.clone, body=%wide.region_2.3_spmd.clone.clone.sunk | while | flops 1042273 | bytes 2474528 | solution.py:87
  210.4 11.3 %broadcast_compare_fusion.66 = (pred[2]{0:T(512)(128)(4,1)S(1)}, pred[2]{0:T(512)(128)(4,1)S(1)}, pred[2]{0:T(512)(128)(4,1)S(1)}, pred[2]{0:T(512)(128)(4,1)S(1...) fusion(s32[2]{0:T(128)S(1)} %get-tuple-element.1511, ...), kind=kLoop, calls=%fused_computation.395.clone.1 | loop fusion | flops 72 | bytes 152 | tf_op jit(solution)/shard_map/while/body/eval_jaxpr/gt | solution.py:77
  236.4 8.8 broadcast_compare_fusion.67
  256.8 11.3 %broadcast_compare_fusion.66 = (pred[2]{0:T(512)(128)(4,1)S(1)}, pred[2]{0:T(512)(128)(4,1)S(1)}, pred[2]{0:T(512)(128)(4,1)S(1)}, pred[2]{0:T(512)(128)(4,1)S(1...) fusion(s32[2]{0:T(128)S(1)} %get-tuple-element.1511, ...), kind=kLoop, calls=%fused_computation.395.clone.1 | loop fusion | flops 72 | bytes 152 | tf_op jit(solution)/shard_map/while/body/eval_jaxpr/gt | solution.py:77
  282.9 8.8 broadcast_compare_fusion.67
  303.3 11.3 %broadcast_compare_fusion.66 = (pred[2]{0:T(512)(128)(4,1)S(1)}, pred[2]{0:T(512)(128)(4,1)S(1)}, pred[2]{0:T(512)(128)(4,1)S(1)}, pred[2]{0:T(512)(128)(4,1)S(1...) fusion(s32[2]{0:T(128)S(1)} %get-tuple-element.1511, ...), kind=kLoop, calls=%fused_computation.395.clone.1 | loop fusion | flops 72 | bytes 152 | tf_op jit(solution)/shard_map/while/body/eval_jaxpr/gt | solution.py:77
  329.3 8.8 broadcast_compare_fusion.67
  349.7 11.3 %broadcast_compare_fusion.66 = (pred[2]{0:T(512)(128)(4,1)S(1)}, pred[2]{0:T(512)(128)(4,1)S(1)}, pred[2]{0:T(512)(128)(4,1)S(1)}, pred[2]{0:T(512)(128)(4,1)S(1...) fusion(s32[2]{0:T(128)S(1)} %get-tuple-element.1511, ...), kind=kLoop, calls=%fused_computation.395.clone.1 | loop fusion | flops 72 | bytes 152 | tf_op jit(solution)/shard_map/while/body/eval_jaxpr/gt | solution.py:77
  375.8 8.8 broadcast_compare_fusion.67
  396.2 11.3 %broadcast_compare_fusion.66 = (pred[2]{0:T(512)(128)(4,1)S(1)}, pred[2]{0:T(512)(128)(4,1)S(1)}, pred[2]{0:T(512)(128)(4,1)S(1)}, pred[2]{0:T(512)(128)(4,1)S(1...) fusion(s32[2]{0:T(128)S(1)} %get-tuple-element.1511, ...), kind=kLoop, calls=%fused_computation.395.clone.1 | loop fusion | flops 72 | bytes 152 | tf_op jit(solution)/shard_map/while/body/eval_jaxpr/gt | solution.py:77
  422.2 8.8 broadcast_compare_fusion.67
  442.6 11.3 %broadcast_compare_fusion.66 = (pred[2]{0:T(512)(128)(4,1)S(1)}, pred[2]{0:T(512)(128)(4,1)S(1)}, pred[2]{0:T(512)(128)(4,1)S(1)}, pred[2]{0:T(512)(128)(4,1)S(1...) fusion(s32[2]{0:T(128)S(1)} %get-tuple-element.1511, ...), kind=kLoop, calls=%fused_computation.395.clone.1 | loop fusion | flops 72 | bytes 152 | tf_op jit(solution)/shard_map/while/body/eval_jaxpr/gt | solution.py:77
  468.6 8.8 broadcast_compare_fusion.67
  489.1 11.3 %broadcast_compare_fusion.66 = (pred[2]{0:T(512)(128)(4,1)S(1)}, pred[2]{0:T(512)(128)(4,1)S(1)}, pred[2]{0:T(512)(128)(4,1)S(1)}, pred[2]{0:T(512)(128)(4,1)S(1...) fusion(s32[2]{0:T(128)S(1)} %get-tuple-element.1511, ...), kind=kLoop, calls=%fused_computation.395.clone.1 | loop fusion | flops 72 | bytes 152 | tf_op jit(solution)/shard_map/while/body/eval_jaxpr/gt | solution.py:77
  515.1 8.8 broadcast_compare_fusion.67
  535.5 11.3 %broadcast_compare_fusion.66 = (pred[2]{0:T(512)(128)(4,1)S(1)}, pred[2]{0:T(512)(128)(4,1)S(1)}, pred[2]{0:T(512)(128)(4,1)S(1)}, pred[2]{0:T(512)(128)(4,1)S(1...) fusion(s32[2]{0:T(128)S(1)} %get-tuple-element.1511, ...), kind=kLoop, calls=%fused_computation.395.clone.1 | loop fusion | flops 72 | bytes 152 | tf_op jit(solution)/shard_map/while/body/eval_jaxpr/gt | solution.py:77
  561.5 8.8 broadcast_compare_fusion.67
  582.0 11.3 %broadcast_compare_fusion.66 = (pred[2]{0:T(512)(128)(4,1)S(1)}, pred[2]{0:T(512)(128)(4,1)S(1)}, pred[2]{0:T(512)(128)(4,1)S(1)}, pred[2]{0:T(512)(128)(4,1)S(1...) fusion(s32[2]{0:T(128)S(1)} %get-tuple-element.1511, ...), kind=kLoop, calls=%fused_computation.395.clone.1 | loop fusion | flops 72 | bytes 152 | tf_op jit(solution)/shard_map/while/body/eval_jaxpr/gt | solution.py:77
  608.0 8.8 broadcast_compare_fusion.67
  628.4 11.3 %broadcast_compare_fusion.66 = (pred[2]{0:T(512)(128)(4,1)S(1)}, pred[2]{0:T(512)(128)(4,1)S(1)}, pred[2]{0:T(512)(128)(4,1)S(1)}, pred[2]{0:T(512)(128)(4,1)S(1...) fusion(s32[2]{0:T(128)S(1)} %get-tuple-element.1511, ...), kind=kLoop, calls=%fused_computation.395.clone.1 | loop fusion | flops 72 | bytes 152 | tf_op jit(solution)/shard_map/while/body/eval_jaxpr/gt | solution.py:77
  654.4 8.8 broadcast_compare_fusion.67
  674.8 11.3 %broadcast_compare_fusion.66 = (pred[2]{0:T(512)(128)(4,1)S(1)}, pred[2]{0:T(512)(128)(4,1)S(1)}, pred[2]{0:T(512)(128)(4,1)S(1)}, pred[2]{0:T(512)(128)(4,1)S(1...) fusion(s32[2]{0:T(128)S(1)} %get-tuple-element.1511, ...), kind=kLoop, calls=%fused_computation.395.clone.1 | loop fusion | flops 72 | bytes 152 | tf_op jit(solution)/shard_map/while/body/eval_jaxpr/gt | solution.py:77
  700.9 8.8 broadcast_compare_fusion.67
  721.3 11.3 %broadcast_compare_fusion.66 = (pred[2]{0:T(512)(128)(4,1)S(1)}, pred[2]{0:T(512)(128)(4,1)S(1)}, pred[2]{0:T(512)(128)(4,1)S(1)}, pred[2]{0:T(512)(128)(4,1)S(1...) fusion(s32[2]{0:T(128)S(1)} %get-tuple-element.1511, ...), kind=kLoop, calls=%fused_computation.395.clone.1 | loop fusion | flops 72 | bytes 152 | tf_op jit(solution)/shard_map/while/body/eval_jaxpr/gt | solution.py:77
  747.3 8.8 broadcast_compare_fusion.67
  767.7 11.3 %broadcast_compare_fusion.66 = (pred[2]{0:T(512)(128)(4,1)S(1)}, pred[2]{0:T(512)(128)(4,1)S(1)}, pred[2]{0:T(512)(128)(4,1)S(1)}, pred[2]{0:T(512)(128)(4,1)S(1...) fusion(s32[2]{0:T(128)S(1)} %get-tuple-element.1511, ...), kind=kLoop, calls=%fused_computation.395.clone.1 | loop fusion | flops 72 | bytes 152 | tf_op jit(solution)/shard_map/while/body/eval_jaxpr/gt | solution.py:77
  793.7 8.8 broadcast_compare_fusion.67
  814.2 11.3 %broadcast_compare_fusion.66 = (pred[2]{0:T(512)(128)(4,1)S(1)}, pred[2]{0:T(512)(128)(4,1)S(1)}, pred[2]{0:T(512)(128)(4,1)S(1)}, pred[2]{0:T(512)(128)(4,1)S(1...) fusion(s32[2]{0:T(128)S(1)} %get-tuple-element.1511, ...), kind=kLoop, calls=%fused_computation.395.clone.1 | loop fusion | flops 72 | bytes 152 | tf_op jit(solution)/shard_map/while/body/eval_jaxpr/gt | solution.py:77
  840.2 8.8 broadcast_compare_fusion.67
  860.6 11.3 %broadcast_compare_fusion.66 = (pred[2]{0:T(512)(128)(4,1)S(1)}, pred[2]{0:T(512)(128)(4,1)S(1)}, pred[2]{0:T(512)(128)(4,1)S(1)}, pred[2]{0:T(512)(128)(4,1)S(1...) fusion(s32[2]{0:T(128)S(1)} %get-tuple-element.1511, ...), kind=kLoop, calls=%fused_computation.395.clone.1 | loop fusion | flops 72 | bytes 152 | tf_op jit(solution)/shard_map/while/body/eval_jaxpr/gt | solution.py:77
  886.7 8.8 broadcast_compare_fusion.67
  907.1 11.3 %broadcast_compare_fusion.66 = (pred[2]{0:T(512)(128)(4,1)S(1)}, pred[2]{0:T(512)(128)(4,1)S(1)}, pred[2]{0:T(512)(128)(4,1)S(1)}, pred[2]{0:T(512)(128)(4,1)S(1...) fusion(s32[2]{0:T(128)S(1)} %get-tuple-element.1511, ...), kind=kLoop, calls=%fused_computation.395.clone.1 | loop fusion | flops 72 | bytes 152 | tf_op jit(solution)/shard_map/while/body/eval_jaxpr/gt | solution.py:77
  933.1 8.8 broadcast_compare_fusion.67
  949.6 11.6 %reduce.2 = f32[256,3072]{1,0:T(8,128)} reduce(f32[256,1,3072]{2,1,0:T(1,128)} %all-to-all-done, f32[]{:T(128)} %broadcast.2932), dimensions={1}, to_apply=%all_to_all.16.reduce_sub_computation | reduce | bytes 6291460 | tf_op jit(solution)/shard_map/all_to_all | solution.py:41
  961.3 14.1 %reshape.1661 = f32[256,2,12,2,2,32]{5,4,3,2,1,0:T(2,128)} reshape(f32[256,3072]{1,0:T(8,128)} %reduce.2) | data formatting | bytes 6291456
  975.4 18.2 %copy.67 = f32[4,64,2,32,12,2,2]{1,0,3,6,5,4,2:T(4,128)} copy(f32[4,64,2,32,12,2,2]{3,6,5,4,2,1,0:T(2,128)} %bitcast.543) | data formatting | bytes 6291456 | tf_op jit(solution)/shard_map/reshape | solution.py:42
  1014.1 11.0 %copy.65 = f32[512,32,128,1]{2,1,3,0:T(8,128)} copy(f32[512,32,128,1]{0,1,2,3:T(8,128)} %bitcast.549) | data formatting | bytes 16777216 | tf_op jit(solution)/shard_map/all_gather | solution.py:157
  1025.1 15.9 %convolution_bitcast_fusion = f32[2,2,32,512]{2,1,0,3:T(2,128)S(1)} fusion(f32[512,32,128,1]{2,1,3,0:T(8,128)} %copy.65, f32[128,2,2,512]{0,3,2,1:T(8,128)S(1)} %fusion.131), kind=kOutput, calls=%fused_computation.442 | convolution fusion | flops 100663296 | bytes 9699328 | tf_op jit(solution)/shard_map/rocl,lnr->ocnl/dot_general | solution.py:154
  1041.9 11.1 %all_to_all.23 = f32[2,2,32,512]{3,1,0,2:T(2,128)S(1)} all-to-all(f32[2,2,32,512]{3,1,0,2:T(2,128)S(1)} %copy.59), channel_id=1, replica_groups=mesh['rad'=4,'lat'=64] {'rad'}, dimensions={2} | all-to-all | bytes 524288 | tf_op jit(solution)/shard_map/all_to_all | solution.py:160
  (846 shorter events, 151.0 us)
Async XLA Ops:
  6.5 3.0 copy-start.7
  6.5 3.0 copy-start.8
  6.5 1007.5 %all-gather.2.cloned.1.call-start = ((), (), s32[]{:S(2)}) async-start(), calls=%async_computation.2 | async-start | bytes 10485760 | tf_op jit(solution)/shard_map/all_gather | solution.py:157
  12.0 1.4 copy-start
  12.0 10.8 %copy-start.3 = (f32[512,32,32]{0,2,1:T(8,128)S(1)}, f32[512,32,32]{0,2,1:T(8,128)}, u32[]{:S(2)}) copy-start(f32[512,32,32]{0,2,1:T(8,128)} %param.15) | copy-start | bytes 6291460
  13.4 42.4 %collective-permute-start = (f32[2,3,12,1536]{3,0,2,1:T(2,128)S(1)}, f32[2,3,12,1536]{3,0,2,1:T(2,128)S(1)}, u32[]{:S(2)}, u32[]{:S(2)}) collective-permute-start(f32[2,3,12,1536]{3,0,2,1:T(2,128)S(1)} %copy.42), channel_id=1, source_target_pairs={{0,64},{64,128},{128,192},{1,65},{65,129},{129,193},{2,66},{66,130... | collective-permute-start | bytes 1327112 | tf_op jit(solution)/shard_map/ppermute | solution.py:17
  20.7 35.4 %collective-permute-start.1 = (f32[2,3,12,1536]{3,0,2,1:T(2,128)}, f32[2,3,12,1536]{3,0,2,1:T(2,128)}, u32[]{:S(2)}, u32[]{:S(2)}) collective-permute-start(f32[2,3,12,1536]{3,0,2,1:T(2,128)} %copy.43), channel_id=1, source_target_pairs={{64,0},{128,64},{192,128},{65,1},{129,65},{193,129},{66,2},{130,66... | collective-permute-start | bytes 1327112 | tf_op jit(solution)/shard_map/ppermute | solution.py:18
  25.5 14.0 %copy-start.6 = (s32[512]{0:T(512)S(1)}, s32[512]{0:T(512)}, u32[]{:S(2)}) copy-start(s32[512]{0:T(512)} %param.14) | copy-start | bytes 6148
  25.5 16.0 %copy-start.4 = (s32[4]{0:T(128)S(1)}, s32[4]{0:T(128)}, u32[]{:S(2)}) copy-start(s32[4]{0:T(128)} %param.11) | copy-start | bytes 52
  25.5 16.7 %copy-start.5 = (f32[2,4,32]{2,1,0:T(4,128)S(1)}, f32[2,4,32]{2,1,0:T(4,128)}, u32[]{:S(2)}) copy-start(f32[2,4,32]{2,1,0:T(4,128)} %param.12) | copy-start | bytes 3076
  49.3 8.1 copy-start.1
  60.5 13.3 %copy-start.2 = (f32[1,32,12,1536]{3,1,2,0:T(8,128)S(1)}, f32[1,32,12,1536]{3,1,2,0:T(8,128)}, u32[]{:S(2)}) copy-start(f32[1,32,12,1536]{3,1,2,0:T(8,128)} %get-tuple-element.832) | copy-start | bytes 7077892
  186.9 762.2 %all-to-all-start = ((f32[256,1,3072]{2,1,0:T(1,128)}), f32[256,1,3072]{2,1,0:T(1,128)}, u32[]{:S(2)}, u32[]{:S(2)}) async-start(f32[256,1,3072]{2,1,0:T(1,128)} %reshape.1660), calls=%async_computation | async-start | bytes 6291456 | tf_op jit(solution)/shard_map/all_to_all | solution.py:41
Sparse Core Ops, SparseCore 0:
  25.5 68.1 all-gather.1
where the time goes:
time: 1070 us; the launch traced here: 1060 us
  other arithmetic  450 us (42%)
  loops' own time  331 us (31%)
  local copies, waits for them, and re-layouts  184 us (17%)
  matrix products  42.4 us (4%)
  starting transfers between devices  23.8 us (2%)
  between operations  19.2 us (2%)
  blocking collectives  11.1 us (1%)
    another operation x1, loops' own time, legendre_rows(): lax.scan(advance, (zeros, zeros, zeros), jnp.arange(degrees, dtype=jnp.in...  331 us
    gt x32, other arithmetic, advance(): degree > orders  322 us
    while x512, other arithmetic  48.1 us
    gather x1, local copies, waits for them, and re-layouts, body(): by_slot = jnp.take(spectrum, slot_order, axis=4)  36 us
    unnamed x21, local copies, waits for them, and re-layouts  32.9 us
    slice x32, local copies, waits for them, and re-layouts, legendre_rows(): lax.scan(advance, (zeros, zeros, zeros), jnp.arange(degrees, dtype=jnp.in...  22.8 us
  transfers between devices with their start and end apart: 4, of which 0 were waited for; matrix products, arithmetic and copies ran while one was open for 60% of the time, Pallas kernels for 0%

commit v1 on v0

v1 whole, which is shorter than its diff:
```python
import functools
import math

import jax
import jax.numpy as jnp
import numpy as np
from jax import lax
from jax.experimental import pallas as pl
from jax.experimental.pallas import tpu as pltpu
from jax.sharding import PartitionSpec as P

TAPS = 4
HALO = 3
LANES = 128
LEVEL = 60.0


def master_tables(lon, degrees):
    half = lon // 2
    orders = np.arange(degrees).reshape(degrees // 2, 2).T
    angle = (2.0 * np.pi / lon) * ((orders[:, :, None] * np.arange(half)) % lon)
    full = np.stack([np.cos(angle), -np.sin(angle)], axis=1) / math.sqrt(lon)
    high = full.astype(np.float32).astype(jnp.bfloat16)
    low = (full - high.astype(np.float64)).astype(np.float32).astype(jnp.bfloat16)
    return np.concatenate([high, low], axis=1)


def split(x):
    high = x.astype(jnp.bfloat16)
    return high, (x - high.astype(jnp.float32)).astype(jnp.bfloat16)


def gather_kernel(row_ref, table_ref, out_ref):
    count = table_ref.shape[2]
    hot = row_ref[0] == lax.broadcasted_iota(jnp.int32, (count, count), 1)
    out_ref[0, 0] = jnp.dot(
        hot.astype(jnp.bfloat16), table_ref[0, 0], preferred_element_type=jnp.float32
    ).astype(jnp.bfloat16)


def gathered_tables(rows, tables):
    _, kinds, count, half = tables.shape
    return pl.pallas_call(
        gather_kernel,
        grid=(2, kinds),
        in_specs=[
            pl.BlockSpec((1, count, 1), lambda p, k: (p, 0, 0)),
            pl.BlockSpec((1, 1, count, half), lambda p, k: (p, k, 0, 0)),
        ],
        out_specs=pl.BlockSpec((1, 1, count, half), lambda p, k: (p, k, 0, 0)),
        out_shape=jax.ShapeDtypeStruct(tables.shape, jnp.bfloat16),
        name="gather_rows",
    )(rows[:, :, None], tables)


def fourier_kernel(
    off_ref, rho_ref, w_ref, ang_ref, v_ref, lo_ref, hi_ref, t_ref, y_ref, c_ref, g_ref
):
    shells, lats, lon = v_ref.shape[1:]
    half = lon // 2
    pitch = 16
    step = half // 2
    c_ref[:, 0:HALO] = lo_ref[...]
    c_ref[:, HALO + shells :] = hi_ref[...]

    def store_folded(field, r, col, a, b):
        rows = pl.ds(pl.multiple_of(r * pitch, pitch), lats)
        for i in range(step // LANES):
            lane = slice(i * LANES, (i + 1) * LANES)
            g_ref[0, field, col * (step // LANES) + i, rows] = (a + b)[:, lane]
            g_ref[1, field, col * (step // LANES) + i, rows] = (a - b)[:, lane]

    def first(r, _):
        rho = rho_ref[r]
        scale = ang_ref[r] * rho
        for col in range(2):
            terms = []
            for part in range(2):
                cols = slice(part * half + col * step, part * half + (col + 1) * step)
                radial = v_ref[0, r, :, cols].astype(jnp.float32)
                polar = v_ref[1, r, :, cols].astype(jnp.float32)
                azimuth = v_ref[2, r, :, cols].astype(jnp.float32)
                flux = rho * radial
                c_ref[0, r + HALO, :, cols] = flux * polar
                c_ref[1, r + HALO, :, cols] = flux * azimuth
                terms.append(
                    scale
                    * (
                        polar * polar
                        + azimuth * azimuth
                        - 2.0 * radial * radial
                        + polar * azimuth
                    )
                )
            store_folded(1, r, col, *terms)
        return 0

    lax.fori_loop(0, shells, first, 0)

    def second(r, _):
        for col in range(2):
            terms = []
            for part in range(2):
                cols = slice(part * half + col * step, part * half + (col + 1) * step)
                total = jnp.zeros((lats, step), jnp.float32)
                for tap in range(TAPS):
                    at = r + HALO + off_ref[tap]
                    total = (
                        total
                        + w_ref[0, tap, r] * c_ref[0, at, :, cols]
                        + w_ref[1, tap, r] * c_ref[1, at, :, cols]
                    )
                terms.append(total)
            store_folded(0, r, col, *terms)
        return 0

    lax.fori_loop(0, shells, second, 0)

    count = t_ref.shape[2]
    group = 4
    nt = (((1,), (1,)), ((), ()))
    upper = (lax.broadcasted_iota(jnp.int32, (count, LANES), 0) & 7) < 4
    for block in range(lats // group):
        sums = []
        for parity in range(2):
            rows = []
            for j in range(block * group, (block + 1) * group):
                for field in range(2):
                    rows.append(
                        jnp.concatenate(
                            [
                                g_ref[parity, field, i, pl.ds(j, shells, stride=pitch), :]
                                for i in range(half // LANES)
                            ],
                            axis=1,
                        )
                    )
            high, low = split(jnp.concatenate(rows, axis=0))
            table = t_ref[parity].reshape(4 * count, half)
            main = lax.dot_general(table, high, nt, preferred_element_type=jnp.float32)
            rest = lax.dot_general(
                table[: 2 * count], low, nt, preferred_element_type=jnp.float32
            )
            sums.append(main[: 2 * count] + main[2 * count :] + rest)
        for j in range(group):
            cols = slice(j * 64, (j + 1) * 64)
            even, odd = (
                jnp.concatenate([s[:count, cols], s[count:, cols]], axis=1) for s in sums
            )
            tiles = (count // 8, 8, LANES)
            y_ref[:, 0, block * group + j] = jnp.where(upper, even, odd).reshape(tiles)
            y_ref[:, 1, block * group + j] = jnp.where(upper, odd, even).reshape(tiles)


def fourier(offsets, density, weights, angular, velocity, below, above, tables):
    _, shells, lats, lon = velocity.shape
    count = tables.shape[2]
    smem = pl.BlockSpec(memory_space=pltpu.SMEM)
    vmem = pl.BlockSpec(memory_space=pltpu.VMEM)
    return pl.pallas_call(
        fourier_kernel,
        in_specs=[smem] * 4 + [vmem] * 4,
        out_specs=vmem,
        out_shape=jax.ShapeDtypeStruct((count // 8, 2, lats, 8, LANES), jnp.float32),
        scratch_shapes=[
            pltpu.VMEM((2, shells + 2 * HALO, lats, lon), jnp.float32),
            pltpu.VMEM((2, 2, lon // 2 // LANES, shells * 16, LANES), jnp.float32),
        ],
        name="fourier",
    )(offsets, density, weights, angular, velocity, below, above, tables)


def legendre_kernel(inv_ref, m_ref, start_ref, trig_ref, out_ref, s_ref, p_ref, z_ref, e_ref, f_ref):
    block = out_ref.shape[1] // 8
    lat_count = trig_ref.shape[1]
    base = pl.program_id(0) * block
    wide = lat_count // LANES
    order = jnp.broadcast_to(m_ref[...], (8, LANES))
    quantum = LEVEL * math.log(2.0)

    def columns(i):
        return slice(i * LANES, (i + 1) * LANES)

    @pl.when(pl.program_id(0) == 0)
    def _():
        start = jnp.broadcast_to(start_ref[...], (8, LANES))
        for i in range(wide):
            log_value = start + order * trig_ref[1:2, columns(i)]
            level = jnp.minimum(jnp.ceil(log_value * (1.0 / quantum)), 0.0)
            z_ref[:, columns(i)] = (
                jnp.exp(log_value - level * quantum) * trig_ref[2:3, columns(i)]
            )
            e_ref[:, columns(i)] = level
        zero = jnp.zeros((8, lat_count), jnp.float32)
        s_ref[...] = zero
        p_ref[...] = zero

    def eight(chunk, _):
        levels, scales, current, older = [], [], [], []
        for i in range(wide):
            s = s_ref[:, columns(i)]
            p = p_ref[:, columns(i)]
            e = e_ref[:, columns(i)]
            grow = (jnp.maximum(jnp.abs(s), jnp.abs(p)) > 1.0) & (e < 0.0)
            shrink = jnp.where(grow, 2.0**-LEVEL, 1.0)
            e = e + jnp.where(grow, 1.0, 0.0)
            e_ref[:, columns(i)] = e
            current.append(s * shrink)
            older.append(p * shrink)
            scales.append(
                jnp.where(
                    e > -0.5,
                    1.0,
                    jnp.where(e > -1.5, 2.0**-LEVEL, jnp.where(e > -2.5, 2.0 ** (-2 * LEVEL), 0.0)),
                )
            )
        first = base + chunk * 8
        before = jnp.maximum(first - 1, 0)
        before_f = before.astype(jnp.float32)
        back = jnp.maximum((before_f * before_f - order * order) * inv_ref[before], 1e-7)
        back = jnp.sqrt(back)
        for step in range(8):
            degree = first + step
            level = degree.astype(jnp.float32)
            ratio = jnp.maximum((level * level - order * order) * inv_ref[degree], 1e-7)
            up = lax.rsqrt(ratio)
            up_back = up * back
            back = ratio * up
            starting = order == level
            for i in range(wide):
                entry = jnp.where(starting, z_ref[:, columns(i)], 0.0) - up_back * older[i]
                value = (up * trig_ref[0:1, columns(i)]) * current[i] + entry
                older[i] = current[i]
                current[i] = value
                row = pl.multiple_of((chunk * 8 + step) * 8, 8)
                out_ref[i, pl.ds(row, 8), :] = value * scales[i]
        for i in range(wide):
            s_ref[:, columns(i)] = current[i]
            p_ref[:, columns(i)] = older[i]
        return 0

    lax.fori_loop(0, block // 8, eight, 0)


def legendre_table(orders, lat_count, degrees):
    colatitude = np.pi * (np.arange(lat_count) + 0.5) / lat_count
    sine = np.sin(colatitude)
    trig = np.stack(
        [np.cos(colatitude), np.log(sine), math.sqrt(np.pi / lat_count) * sine]
    ).astype(np.float32)
    ladder = np.arange(1, degrees)
    logs = 0.5 * math.log(0.5) + np.concatenate(
        [[0.0], np.cumsum(0.5 * np.log((2.0 * ladder + 1.0) / (2.0 * ladder)))]
    )
    level = np.arange(degrees, dtype=np.float64)
    inverse = (1.0 / np.maximum(4.0 * level * level - 1.0, 1.0)).astype(np.float32)
    start = jnp.take(jnp.asarray(logs, jnp.float32), orders)[:, None]
    block = 64
    vmem = pl.BlockSpec(memory_space=pltpu.VMEM)
    return pl.pallas_call(
        legendre_kernel,
        grid=(degrees // block,),
        in_specs=[pl.BlockSpec(memory_space=pltpu.SMEM), vmem, vmem, vmem],
        out_specs=pl.BlockSpec((lat_count // LANES, block * 8, LANES), lambda i: (0, i, 0)),
        out_shape=jax.ShapeDtypeStruct((lat_count // LANES, degrees * 8, LANES), jnp.float32),
        scratch_shapes=[pltpu.VMEM((8, lat_count), jnp.float32)] * 5,
        name="legendre_table",
    )(inverse, orders.astype(jnp.float32)[:, None], start, trig)


def project_kernel(m_ref, slot_ref, z_ref, t_ref, e_ref, out_ref, s_ref):
    wide = t_ref.shape[0]
    block = t_ref.shape[1] // 8
    lat_count = wide * LANES
    shells, modes = e_ref.shape[:2]
    base = pl.program_id(0) * block
    degree = (base + lax.broadcasted_iota(jnp.int32, (block, LANES), 0)).astype(jnp.float32)
    factor = degree * (degree + 1.0)
    for o in range(8):
        active = m_ref[o] < base + block

        @pl.when(active)
        def _(o=o):
            data_high, data_low = split(z_ref[pl.ds(o, lat_count, stride=8), :])
            rows = jnp.concatenate(
                [t_ref[i, pl.ds(o, block, stride=8), :] for i in range(wide)],
                axis=1,
            )
            high, low = split(rows)
            both = jnp.dot(high, data_high, preferred_element_type=jnp.float32)
            both += jnp.dot(low, data_high, preferred_element_type=jnp.float32)
            both += jnp.dot(high, data_low, preferred_element_type=jnp.float32)
            other = pltpu.roll(both, LANES - shells, 1)
            s_ref[o] = (both - factor * other).T

        @pl.when(jnp.logical_not(active))
        def _(o=o):
            s_ref[o] = jnp.zeros((LANES, block), jnp.float32)

    def project(pair, _):
        totals = [[jnp.zeros((modes, block), jnp.float32) for _ in range(2)] for _ in range(2)]
        for r in range(shells):
            eigen = e_ref[r]
            for a in range(2):
                for part in range(2):
                    row = s_ref[pair * 2 + a, part * 2 * shells + r : part * 2 * shells + r + 1, :]
                    totals[a][part] = totals[a][part] + eigen * row
        quarter = modes // 4
        for a in range(2):
            slot = slot_ref[pair * 2 + a]
            for part in range(2):
                for q in range(4):
                    out_ref[q, slot, part] = totals[a][part][q * quarter : (q + 1) * quarter]
        return 0

    lax.fori_loop(0, 4, project, 0)


def projected(orders, slots, spectrum, table, eigen):
    wide = table.shape[0]
    lat_count = wide * LANES
    shells, modes, degrees = eigen.shape
    block = LANES
    smem = pl.BlockSpec(memory_space=pltpu.SMEM)
    return pl.pallas_call(
        project_kernel,
        grid=(degrees // block,),
        in_specs=[
            smem,
            smem,
            pl.BlockSpec(memory_space=pltpu.VMEM),
            pl.BlockSpec((wide, block * 8, LANES), lambda i: (0, i, 0)),
            pl.BlockSpec((shells, modes, block), lambda i: (0, 0, i)),
        ],
        out_specs=pl.BlockSpec((4, 8, 2, modes // 4, block), lambda i: (0, 0, 0, 0, i)),
        out_shape=jax.ShapeDtypeStruct((4, 8, 2, modes // 4, degrees), jnp.float32),
        scratch_shapes=[pltpu.VMEM((8, LANES, block), jnp.float32)],
        name="project",
    )(orders, slots, spectrum.reshape(lat_count * 8, LANES), table, eigen)


def body(velocity, density, offsets, radial_weights, angular_scale, order_table, eigenfunctions):
    shells, lats, lon = velocity.shape[1:]
    degrees = order_table.shape[0]
    groups = lax.axis_size("lat")
    lat_count = lats * groups
    where = lax.axis_index("lat")

    def cross(part):
        flow, rho = part
        flow = flow.astype(jnp.float32)
        flux = rho[:, None, None] * flow[0]
        return jnp.stack([flux * flow[1], flux * flow[2]])

    size = lax.axis_size("rad")
    up = [(i, i + 1) for i in range(size - 1)]
    down = [(j, i) for i, j in up]
    below = lax.ppermute(cross((velocity[:, shells - HALO :], density[shells - HALO :])), "rad", up)
    above = lax.ppermute(cross((velocity[:, :HALO], density[:HALO])), "rad", down)

    pairs = order_table.reshape(degrees // 2, 2)
    first_even = (pairs[:, 0] & 1) == 0
    even = jnp.where(first_even, pairs[:, 0], pairs[:, 1])
    odd = jnp.where(first_even, pairs[:, 1], pairs[:, 0])
    swapped = odd.reshape(-1, 2, 4)[:, ::-1].reshape(-1)
    tables = gathered_tables(jnp.stack([even, swapped]) >> 1, master_tables(lon, degrees))
    by_slot = fourier(
        offsets, density, radial_weights, angular_scale, velocity, below, above, tables
    )
    by_slot = by_slot.reshape(groups, lats, 8, LANES)
    gathered = lax.all_to_all(by_slot, "lat", split_axis=0, concat_axis=0, tiled=True)

    mine = lax.dynamic_slice_in_dim(pairs, where * 4, 4)
    flip = (mine[:, 0] & 1) ^ (where & 1)
    flip = flip[None, :] ^ jnp.arange(2, dtype=jnp.int32)[:, None]
    orders = jnp.where(flip == 0, mine[None, :, 0], mine[None, :, 1]).reshape(8)
    slots = (2 * jnp.arange(4, dtype=jnp.int32)[None, :] + flip).reshape(8)
    table = legendre_table(orders, lat_count, degrees)
    eigen = jnp.transpose(eigenfunctions, (2, 1, 0))
    partial = projected(orders, slots, gathered.reshape(lat_count, 8, LANES), table, eigen)
    return lax.all_to_all(partial, "rad", split_axis=0, concat_axis=0, tiled=True).sum(0)


def solution(mesh):
    placed = (
        P(None, "rad", "lat", None),
        P("rad"),
        P(),
        P(None, None, "rad"),
        P("rad"),
        P(),
        P(None, None, "rad"),
    )
    return jax.shard_map(
        body, mesh=mesh, in_specs=placed, out_specs=P("lat", None, "rad", None), check_vma=False
    )
```

time: 1070 us -> 177 us (0.17)
  other arithmetic: 450 us -> 8.22 us
  loops' own time: 331 us -> 0 us
  local copies, waits for them, and re-layouts: 184 us -> 23.8 us
  waiting for transfers between devices: 0.05 us -> 54.4 us
  Pallas kernels: 0 us -> 49 us
  matrix products: 42.4 us -> 0 us
  between operations: 19.2 us -> 0.14 us
    another operation x1 -> x0, loops' own time: 331 us -> none  [legendre_rows(): lax.scan(advance, (zeros, zeros, zeros), jnp.arange(degrees, dtype=jnp.in...]
    gt x32 -> x0, other arithmetic: 322 us -> none  [advance(): degree > orders]
    all_to_all x1, waiting for transfers between devices: 0.01 us -> 54.4 us  [body(): lax.all_to_all(by_slot, 'lat', split_axis=0, concat_axis=0, tiled=True)]
    pallas_call x0 -> x4, Pallas kernels: none -> 49 us  [the longest x1 18.3 us: projected(): pl.pallas_call(project_kernel, grid=(degrees // block,), in_specs=[smem,...]
    while x512 -> x0, other arithmetic: 48.1 us -> none
    dot_general x3 -> x0, matrix products: 42.4 us -> none  [the longest x1 19.2 us: body(): jnp.dot(fields, fourier_table(lon_count, degrees), precision=lax.Precisio...]
    gather x2, local copies, waits for them, and re-layouts: 36.6 us -> 0.73 us  [legendre_table(): start = jnp.take(jnp.asarray(logs, jnp.float32), orders)[:, None]]
    reshape x5 -> x1, local copies, waits for them, and re-layouts: 30.1 us -> 0.79 us  [body(): pairs = order_table.reshape(degrees // 2, 2)]
  transfers between devices with their start and end apart: 4 -> 3, of which waited for: 0 -> 1; matrix products, arithmetic and copies ran while one was open for 60% -> 13% of each run, Pallas kernels for 0% -> 9%
where the time goes in v1:
time: 177 us; the launch traced here: 174 us
  waiting for transfers between devices  54.4 us (31%)
  Pallas kernels  49 us (28%)
  local copies, waits for them, and re-layouts  23.8 us (13%)
  starting transfers between devices  19.9 us (11%)
  blocking collectives  18.5 us (10%)
  other arithmetic  8.22 us (5%)
    all_to_all x1, waiting for transfers between devices, body(): lax.all_to_all(by_slot, 'lat', split_axis=0, concat_axis=0, tiled=True)  54.4 us
    all_to_all x1, blocking collectives, body(): lax.all_to_all(partial, 'rad', split_axis=0, concat_axis=0, tiled=True)  18.5 us
    pallas_call x1, Pallas kernels, projected(): pl.pallas_call(project_kernel, grid=(degrees // block,), in_specs=[smem,...  18.3 us
    pallas_call x1, Pallas kernels, fourier(): pl.pallas_call(fourier_kernel, in_specs=[smem] * 4 + [vmem] * 4, out_spec...  14.3 us
    all_to_all x1, starting transfers between devices, body(): lax.all_to_all(by_slot, 'lat', split_axis=0, concat_axis=0, tiled=True)  12 us
    unnamed x10, local copies, waits for them, and re-layouts  9.97 us
    pallas_call x1, Pallas kernels, legendre_table(): pl.pallas_call(legendre_kernel, grid=(degrees // block,), in_specs=[pl.Bl...  9.17 us
    pallas_call x1, Pallas kernels, gathered_tables(): pl.pallas_call(gather_kernel, grid=(2, kinds), in_specs=[pl.BlockSpec((1,...  7.23 us
  transfers between devices with their start and end apart: 3, of which 1 were waited for; matrix products, arithmetic and copies ran while one was open for 13% of the time, Pallas kernels for 9%

profile of v1, /device:TPU:1, one launch (start us, length us, event | category | flops | bytes accessed | tf_op | source)
XLA Modules:
  0.0 174.0 jit_solution(5858291301624445329)
XLA Ops:
  0.0 0.8 fusion.4
  0.8 1.8 %fusion.3 = (bf16[3,3,12,1536]{3,1,2,0:T(4,128)(2,1)S(1)}, bf16[3,3,12,1536]{3,1,2,0:T(4,128)(2,1)S(1)}) fusion(bf16[3,32,12,1536]{3,1,2,0:T(8,128)(2,1)} %param.11), kind=kLoop, calls=%fused_computation.30 | loop fusion | bytes 1327104 | tf_op jit(solution)/shard_map/slice | solution.py:359
  2.6 0.0 copy-start.3
  2.6 0.0 copy-start.2
  2.6 0.7 copy_convert_fusion
  3.3 0.5 slice_multiply_fusion.4
  3.8 1.2 pad_maximum_fusion
  5.0 6.0 %collective-permute-start = (f32[2,3,12,1536]{3,0,2,1:T(2,128)}, f32[2,3,12,1536]{3,0,2,1:T(2,128)}, u32[]{:S(2)}, u32[]{:S(2)}) collective-permute-start(f32[2,3,12,1536]{3,0,2,1:T(2,128)} %pad_maximum_fusion), channel_id=1, source_target_pairs={{0,64},{64,128},{128,192},{1,65},{65,129},{129,193},{2,66},{66,130... | collective-permute-start | bytes 1327112 | tf_op jit(solution)/shard_map/ppermute | solution.py:358
  11.0 0.5 slice_multiply_fusion.1
  11.5 1.2 pad_maximum_fusion.1
  12.6 1.9 %collective-permute-start.1 = (f32[2,3,12,1536]{3,0,2,1:T(2,128)}, f32[2,3,12,1536]{3,0,2,1:T(2,128)}, u32[]{:S(2)}, u32[]{:S(2)}) collective-permute-start(f32[2,3,12,1536]{3,0,2,1:T(2,128)} %pad_maximum_fusion.1), channel_id=1, source_target_pairs={{64,0},{128,64},{192,128},{65,1},{129,65},{193,129},{66,2},{130,66... | collective-permute-start | bytes 1327112 | tf_op jit(solution)/shard_map/ppermute | solution.py:359
  14.5 0.0 copy-done.3
  14.5 0.8 reshape.222
  15.3 1.2 slice_reduce_fusion.1
  16.5 0.7 squeeze.25
  17.3 0.7 squeeze.26
  18.0 1.4 compare_select_fusion
  19.4 0.0 copy-done.2
  19.4 4.2 %copy.61.v_ref = bf16[3,32,12,1536]{3,2,1,0:T(8,128)(2,1)} copy(bf16[3,32,12,1536]{3,1,2,0:T(8,128)(2,1)S(1)} %copy-done.2) | data formatting | bytes 7077888 | tf_op args[0]
  23.6 0.8 rev.3
  24.4 0.1 stack.23
  24.5 0.1 copy.59
  24.7 0.7 add_shift-right-arithmetic_fusion.row_ref
  25.4 7.2 %gather_rows.1.t_ref = bf16[2,4,256,768]{3,2,1,0:T(8,128)(2,1)} custom-call(s32[2,256,1]{2,1,0:T(8,128)} %add_shift-right-arithmetic_fusion.row_ref, bf16[2,4,256,768]{3,2,1,0:T(8,128)(2,1)} %constant.12.clone.table_ref), custom_call_target="tpu_custom_call" | custom-call | tf_op jit(solution)/shard_map/gather_rows/pallas_call | solution.py:43
  32.6 0.0 collective-permute-done
  32.6 2.0 %copy.62.lo_ref = f32[2,3,12,1536]{3,2,1,0:T(8,128)} copy(f32[2,3,12,1536]{3,0,2,1:T(2,128)} %collective-permute-done) | data formatting | bytes 884736 | tf_op jit(solution)/shard_map/ppermute | solution.py:358
  34.6 0.0 collective-permute-done.1
  34.6 2.0 %copy.63.hi_ref = f32[2,3,12,1536]{3,2,1,0:T(8,128)} copy(f32[2,3,12,1536]{3,0,2,1:T(2,128)} %collective-permute-done.1) | data formatting | bytes 884736 | tf_op jit(solution)/shard_map/ppermute | solution.py:359
  36.6 14.3 %fourier.1 = f32[32,2,12,8,128]{4,3,2,1,0:T(8,128)} custom-call(s32[4]{0:T(128)} %off_ref.1, f32[32]{0:T(128)} %rho_ref.1, f32[2,4,32]{2,1,0:T(4,128)} %w_ref.1, f32[32]{0:T(128)} %ang_ref.1, bf16[3,32,12,1536]{3,2,1,0:T(8,128)(2,1)} %copy.61.v_ref, f32[2,3,12,1536]{3,2,1,0:T(8,128)} %copy.62.lo_ref, f32[2,3,12,1536]{3,2,1,0:T(8,128)} %copy.63.hi_ref, ...), custom_call_target="tpu_custom_call" | custom-call | tf_op jit(solution)/shard_map/fourier/pallas_call | solution.py:160
  50.9 0.0 copy-start
  50.9 12.0 %all-to-all-start = ((f32[64,12,8,128]{3,2,1,0:T(8,128)}), f32[64,12,8,128]{3,2,1,0:T(8,128)S(1)}, u32[]{:S(2)}, u32[]{:S(2)}) async-start(f32[64,12,8,128]{3,2,1,0:T(8,128)} %bitcast.11), calls=%async_computation | async-start | bytes 6291456 | tf_op jit(solution)/shard_map/all_to_all | solution.py:371
  62.9 0.7 constant_dynamic-slice_fusion
  63.6 0.2 slice_reduce_fusion.3
  63.8 0.6 select_n.83.m_ref
  64.4 0.1 select_n.89
  64.5 0.6 add.35.slot_ref
  65.0 0.7 fusion
  65.7 0.0 copy-done
  65.8 0.6 gather_fusion
  66.4 0.1 copy.68
  66.5 4.1 %copy.75 = f32[512,32,32]{0,1,2:T(8,128)} copy(f32[512,32,32]{0,2,1:T(8,128)} %param.17) | data formatting | bytes 4194304 | tf_op args[6]
  70.6 0.6 and_select_fusion.start_ref
  71.2 9.2 %legendre_table.1.t_ref = f32[6,4096,128]{2,1,0:T(8,128)} custom-call(f32[512]{0:T(512)} %constant.46.clone.inv_ref, f32[8,1]{1,0:T(8,128)} %get-tuple-element.16.m_ref, f32[8,1]{1,0:T(8,128)} %and_select_fusion.start_ref, f32[3,768]{1,0:T(4,128)} %constant.47.clone.trig_ref), custom_call_target="tpu_custom_call" | custom-call | tf_op jit(solution)/shard_map/legendre_table/pallas_call | solution.py:260
  80.4 54.4 %all-to-all-done = f32[64,12,8,128]{3,2,1,0:T(8,128)S(1)} async-done(((f32[64,12,8,128]{3,2,1,0:T(8,128)}), f32[64,12,8,128]{3,2,1,0:T(8,128)S(1)}, u32[]{:S(2)}, u32[]{:S(2)}) %all-to-all-start) | async-done | bytes 3145760 | tf_op jit(solution)/shard_map/all_to_all | solution.py:371
  134.7 1.7 copy-done.1
  136.4 18.3 %project.1 = f32[4,8,2,8,512]{4,3,2,1,0:T(8,128)} custom-call(s32[8]{0:T(128)} %select_n.83.m_ref, s32[8]{0:T(128)} %add.35.slot_ref, f32[6144,128]{1,0:T(8,128)} %bitcast.10, f32[6,4096,128]{2,1,0:T(8,128)} %legendre_table.1.t_ref, f32[32,32,512]{2,1,0:T(8,128)} %bitcast.12), custom_call_target="tpu_custom_call" | custom-call | tf_op jit(solution)/shard_map/project/pallas_call | solution.py:325
  154.7 18.5 %all_to_all.10 = f32[4,8,2,8,512]{4,3,2,1,0:T(8,128)S(1)} all-to-all(f32[4,8,2,8,512]{4,3,2,1,0:T(8,128)} %project.1), channel_id=1, replica_groups=mesh['rad'=4,'lat'=64] {'rad'}, dimensions={0} | all-to-all | bytes 2097152 | tf_op jit(solution)/shard_map/all_to_all | solution.py:381
  173.2 0.8 reduce_sum.9
  (5 shorter events, 0.0 us)
Async XLA Ops:
  2.6 11.9 %copy-start.3 = (s32[512]{0:T(512)S(1)}, s32[512]{0:T(512)}, u32[]{:S(2)}) copy-start(s32[512]{0:T(512)} %param.16) | copy-start | bytes 6148
  2.6 16.8 %copy-start.2 = (bf16[3,32,12,1536]{3,1,2,0:T(8,128)(2,1)S(1)}, bf16[3,32,12,1536]{3,1,2,0:T(8,128)(2,1)}, u32[]{:S(2)}) copy-start(bf16[3,32,12,1536]{3,1,2,0:T(8,128)(2,1)} %param.11) | copy-start | bytes 10616836
  5.0 27.7 %collective-permute-start = (f32[2,3,12,1536]{3,0,2,1:T(2,128)}, f32[2,3,12,1536]{3,0,2,1:T(2,128)}, u32[]{:S(2)}, u32[]{:S(2)}) collective-permute-start(f32[2,3,12,1536]{3,0,2,1:T(2,128)} %pad_maximum_fusion), channel_id=1, source_target_pairs={{0,64},{64,128},{128,192},{1,65},{65,129},{129,193},{2,66},{66,130... | collective-permute-start | bytes 1327112 | tf_op jit(solution)/shard_map/ppermute | solution.py:358
  12.6 22.0 %collective-permute-start.1 = (f32[2,3,12,1536]{3,0,2,1:T(2,128)}, f32[2,3,12,1536]{3,0,2,1:T(2,128)}, u32[]{:S(2)}, u32[]{:S(2)}) collective-permute-start(f32[2,3,12,1536]{3,0,2,1:T(2,128)} %pad_maximum_fusion.1), channel_id=1, source_target_pairs={{64,0},{128,64},{192,128},{65,1},{129,65},{193,129},{66,2},{130,66... | collective-permute-start | bytes 1327112 | tf_op jit(solution)/shard_map/ppermute | solution.py:359
  50.9 14.9 %copy-start = (f32[512]{0:T(512)S(1)}, f32[512]{0:T(512)}, u32[]{:S(2)}) copy-start(f32[512]{0:T(512)} %constant.13.clone) | copy-start | bytes 6148
  50.9 83.8 %all-to-all-start = ((f32[64,12,8,128]{3,2,1,0:T(8,128)}), f32[64,12,8,128]{3,2,1,0:T(8,128)S(1)}, u32[]{:S(2)}, u32[]{:S(2)}) async-start(f32[64,12,8,128]{3,2,1,0:T(8,128)} %bitcast.11), calls=%async_computation | async-start | bytes 6291456 | tf_op jit(solution)/shard_map/all_to_all | solution.py:371
  134.7 1.7 copy-start.1

commit v2 on v1

v2 whole, which is shorter than its diff:
```python
import functools
import math

import jax
import jax.numpy as jnp
import numpy as np
from jax import lax
from jax.experimental import pallas as pl
from jax.experimental.pallas import tpu as pltpu
from jax.sharding import PartitionSpec as P

TAPS = 4
HALO = 3
LANES = 128
LEVEL = 60.0


def master_tables(lon, degrees):
    half = lon // 2
    orders = np.arange(degrees).reshape(degrees // 2, 2).T
    angle = (2.0 * np.pi / lon) * ((orders[:, :, None] * np.arange(half)) % lon)
    full = np.stack([np.cos(angle), -np.sin(angle)], axis=1) / math.sqrt(lon)
    high = full.astype(np.float32).astype(jnp.bfloat16)
    low = (full - high.astype(np.float64)).astype(np.float32).astype(jnp.bfloat16)
    return np.concatenate([high, low], axis=1)


def split(x):
    high = x.astype(jnp.bfloat16)
    return high, (x - high.astype(jnp.float32)).astype(jnp.bfloat16)


def gather_kernel(first_ref, table_ref, out_ref):
    kinds, count = table_ref.shape[1:3]
    parity = pl.program_id(0)
    first = first_ref[...]
    even = jnp.where((first & 1) == 0, first, 2 * count - 1 - first)
    odd = 2 * count - 1 - even
    lane = lax.broadcasted_iota(jnp.int32, (1, count), 1)
    swapped = jnp.where((lane & 4) == 0, pltpu.roll(odd, count - 4, 1), pltpu.roll(odd, 4, 1))
    row = jnp.where(parity == 0, even, swapped) >> 1
    hot = (lax.broadcasted_iota(jnp.int32, (count, count), 0) == row).astype(jnp.float32)
    hot = hot.T.astype(jnp.bfloat16)
    for kind in range(kinds):
        out_ref[0, kind] = jnp.dot(
            hot, table_ref[0, kind], preferred_element_type=jnp.float32
        ).astype(jnp.bfloat16)


def gathered_tables(first, tables):
    block = pl.BlockSpec((1,) + tables.shape[1:], lambda p: (p, 0, 0, 0))
    return pl.pallas_call(
        gather_kernel,
        grid=(2,),
        in_specs=[pl.BlockSpec(memory_space=pltpu.VMEM), block],
        out_specs=block,
        out_shape=jax.ShapeDtypeStruct(tables.shape, jnp.bfloat16),
        name="gather_rows",
    )(first, tables)


def halo_kernel(rho_ref, v_ref, top_ref, bottom_ref, flow_ref, sem):
    lats, shells, lon = v_ref.shape[1:]
    starts = (shells - 8, 0)
    copies = [
        pltpu.make_async_copy(v_ref.at[:, :, pl.ds(start, 8)], flow_ref.at[i], sem.at[i])
        for i, start in enumerate(starts)
    ]
    for copy in copies:
        copy.start()
    wide = lon // LANES
    row = lax.broadcasted_iota(jnp.int32, (8, LANES), 0)
    for i, (start, out_ref) in enumerate(zip(starts, (top_ref, bottom_ref))):
        skip = 8 - HALO if i == 0 else 0
        rho = jnp.zeros((8, LANES), jnp.float32)
        for h in range(8):
            rho = jnp.where(row == h, rho_ref[start + h], rho)
        copies[i].wait()

        def band(lat, _, i=i, rho=rho, out_ref=out_ref, skip=skip):
            for c in range(wide):
                cols = slice(c * LANES, (c + 1) * LANES)
                radial, polar, azimuth = (
                    flow_ref[i, k, lat, :, cols].astype(jnp.float32) for k in range(3)
                )
                flux = rho * radial
                for k, value in enumerate((flux * polar, flux * azimuth)):
                    for h in range(HALO):
                        out_ref[k, h, pl.ds(lat * wide + c, 1)] = value[skip + h : skip + h + 1]
            return 0

        lax.fori_loop(0, lats, band, 0)


def halo_cross(density, velocity):
    _, lats, shells, lon = velocity.shape
    vmem = pl.BlockSpec(memory_space=pltpu.VMEM)
    shape = jax.ShapeDtypeStruct((2, HALO, lats * lon // LANES, LANES), jnp.float32)
    return pl.pallas_call(
        halo_kernel,
        in_specs=[pl.BlockSpec(memory_space=pltpu.SMEM), pl.BlockSpec(memory_space=pl.ANY)],
        out_specs=[vmem, vmem],
        out_shape=[shape, shape],
        scratch_shapes=[
            pltpu.VMEM((2, 3, lats, 8, lon), jnp.bfloat16),
            pltpu.SemaphoreType.DMA((2,)),
        ],
        name="halo_cross",
    )(density, velocity)


CHUNK = 2


def chunk_copy(v_ref, flow_ref, sem, i):
    part = pl.ds(i * CHUNK, CHUNK)
    return pltpu.make_async_copy(v_ref.at[:, part], flow_ref.at[:, part], sem.at[i])


def start_chunks(v_ref, flow_ref, sem):
    for i in range(v_ref.shape[1] // CHUNK):
        chunk_copy(v_ref, flow_ref, sem, i).start()


def wait_chunk(v_ref, flow_ref, sem, lat):
    @pl.when(lat % CHUNK == 0)
    def _():
        chunk_copy(v_ref, flow_ref, sem, lat // CHUNK).wait()


def shell_rows(count, value):
    row = lax.broadcasted_iota(jnp.int32, (8, LANES), 0)
    tiles = []
    for base in range(0, count, 8):
        tile = jnp.zeros((8, LANES), jnp.float32)
        for h in range(8):
            tile = jnp.where(row == h, value(base + h), tile)
        tiles.append(tile)
    return jnp.concatenate(tiles, axis=0)


def store_folded(g_ref, lat, shells, chunk, a, b):
    place = (lat & ~3) + ((lat & 1) << 1) + ((lat & 2) >> 1)
    rows = pl.ds(pl.multiple_of(place * shells, shells), shells)
    cols = slice(chunk * LANES, (chunk + 1) * LANES)
    for parity, value in enumerate((a + b, a - b)):
        high, low = split(value)
        g_ref[parity, 0, rows, cols] = high
        g_ref[parity, 1, rows, cols] = low


def transform(g_ref, t_ref, shells, lats, emit):
    kinds, count, half = t_ref.shape[1:]
    nt = (((1,), (1,)), ((), ()))
    row = lax.broadcasted_iota(jnp.int32, (count, LANES), 0)
    lane = lax.broadcasted_iota(jnp.int32, (count, LANES), 1)
    upper = (row & 7) < 4
    straight = (lane & shells) == 0
    for start, size in ((0, 8), (8, 4)):
        rows = slice(start * shells, (start + size) * shells)
        sums = []
        for parity in range(2):
            table = t_ref[parity].reshape(kinds * count, half)
            high, low = g_ref[parity, 0, rows], g_ref[parity, 1, rows]
            if size == 8:
                main = lax.dot_general(table, high, nt, preferred_element_type=jnp.float32)
                rest = lax.dot_general(
                    table[: 2 * count], low, nt, preferred_element_type=jnp.float32
                )
                sums.append(main[: 2 * count] + main[2 * count :] + rest)
            else:
                both = jnp.concatenate([high, low], axis=0)
                main = lax.dot_general(table, both, nt, preferred_element_type=jnp.float32)
                width = size * shells
                sums.append(
                    main[: 2 * count, :width]
                    + (main[: 2 * count, width:] + main[2 * count :, :width])
                )
        for base in range(0, size, 4):
            cols = slice(base * shells, base * shells + LANES)
            found = []
            for total in sums:
                cosine, sine = total[:count, cols], total[count:, cols]
                found.append(
                    (
                        jnp.where(straight, cosine, pltpu.roll(sine, shells, 1)),
                        jnp.where(straight, pltpu.roll(cosine, LANES - shells, 1), sine),
                    )
                )
            for i in range(2):
                even, odd = found[0][i], found[1][i]
                tiles = (count // 8, 8, LANES)
                emit(
                    (start + base) // 2 + i,
                    jnp.where(upper, even, odd).reshape(tiles),
                    jnp.where(upper, odd, even).reshape(tiles),
                )


def angular_kernel(rho_ref, ang_ref, v_ref, t_ref, a_ref, flow_ref, g_ref, sem):
    lats, shells, lon = v_ref.shape[1:]
    wide = lon // LANES
    start_chunks(v_ref, flow_ref, sem)
    scale = shell_rows(shells, lambda r: ang_ref[r] * rho_ref[r])

    def band(lat, _):
        wait_chunk(v_ref, flow_ref, sem, lat)
        for chunk in range(wide // 2):
            terms = []
            for c in (chunk, chunk + wide // 2):
                cols = slice(c * LANES, (c + 1) * LANES)
                radial, polar, azimuth = (
                    flow_ref[k, lat, :, cols].astype(jnp.float32) for k in range(3)
                )
                terms.append(
                    scale
                    * (
                        polar * polar
                        + azimuth * azimuth
                        - 2.0 * radial * radial
                        + polar * azimuth
                    )
                )
            store_folded(g_ref, lat, shells, chunk, *terms)
        return 0

    lax.fori_loop(0, lats, band, 0)

    def emit(pair, left, right):
        a_ref[:, 0, pair] = left
        a_ref[:, 1, pair] = right

    transform(g_ref, t_ref, shells, lats, emit)


def radial_kernel(
    off_ref, rho_ref, w_ref, v_ref, lo_ref, hi_ref, t_ref, a_ref, y_ref, flow_ref, w_rows, c_ref, g_ref, sem
):
    lats, shells, lon = v_ref.shape[1:]
    wide = lon // LANES
    plane = lats * wide
    start_chunks(v_ref, flow_ref, sem)
    rho = shell_rows(shells, lambda r: rho_ref[r])
    for tap in range(TAPS):
        for k in range(2):
            w_rows[k, tap] = shell_rows(shells, lambda r: w_ref[k, tap, r])

    def band(lat, _):
        wait_chunk(v_ref, flow_ref, sem, lat)
        for c in range(wide):
            cols = slice(c * LANES, (c + 1) * LANES)
            radial, polar, azimuth = (
                flow_ref[k, lat, :, cols].astype(jnp.float32) for k in range(3)
            )
            flux = rho * radial
            c_ref[0, c, 8 : 8 + shells] = flux * polar
            c_ref[1, c, 8 : 8 + shells] = flux * azimuth
            for k in range(2):
                at = pl.ds(k * HALO * plane + lat * wide + c, HALO, stride=plane)
                c_ref[k, c, 8 - HALO : 8] = lo_ref[at, :]
                c_ref[k, c, 8 + shells : 8 + shells + HALO] = hi_ref[at, :]
        for chunk in range(wide // 2):
            terms = []
            for c in (chunk, chunk + wide // 2):
                total = jnp.zeros((shells, LANES), jnp.float32)
                for tap in range(TAPS):
                    at = pl.ds(8 + off_ref[tap], shells)
                    total = (
                        total
                        + w_rows[0, tap] * c_ref[0, c, at, :]
                        + w_rows[1, tap] * c_ref[1, c, at, :]
                    )
                terms.append(total)
            store_folded(g_ref, lat, shells, chunk, *terms)
        return 0

    lax.fori_loop(0, lats, band, 0)

    near = lax.broadcasted_iota(jnp.int32, y_ref.shape[:1] + (8, LANES), 2) < LANES // 2

    def emit(pair, *both):
        for i, mine in enumerate(both):
            other = a_ref[:, i, pair]
            y_ref[:, i, 2 * pair] = jnp.where(near, mine, pltpu.roll(other, LANES // 2, 2))
            y_ref[:, i, 2 * pair + 1] = jnp.where(near, pltpu.roll(mine, LANES // 2, 2), other)

    transform(g_ref, t_ref, shells, lats, emit)


def fourier(offsets, density, weights, angular, velocity, below, above, tables):
    _, lats, shells, lon = velocity.shape
    count = tables.shape[2]
    smem = pl.BlockSpec(memory_space=pltpu.SMEM)
    vmem = pl.BlockSpec(memory_space=pltpu.VMEM)
    hbm = pl.BlockSpec(memory_space=pl.ANY)
    flow = pltpu.VMEM(velocity.shape, velocity.dtype)
    folded = pltpu.VMEM((2, 2, lats * shells, lon // 2), jnp.bfloat16)
    sems = pltpu.SemaphoreType.DMA((lats // CHUNK,))
    ready = pl.pallas_call(
        angular_kernel,
        in_specs=[smem, smem, hbm, vmem],
        out_specs=vmem,
        out_shape=jax.ShapeDtypeStruct((count // 8, 2, lats // 2, 8, LANES), jnp.float32),
        scratch_shapes=[flow, folded, sems],
        name="angular",
    )(density, angular, velocity, tables)
    return pl.pallas_call(
        radial_kernel,
        in_specs=[smem] * 3 + [hbm] + [vmem] * 4,
        out_specs=vmem,
        out_shape=jax.ShapeDtypeStruct((count // 8, 2, lats, 8, LANES), jnp.float32),
        scratch_shapes=[
            flow,
            pltpu.VMEM((2, TAPS, shells, LANES), jnp.float32),
            pltpu.VMEM((2, lon // LANES, shells + 16, LANES), jnp.float32),
            folded,
            sems,
        ],
        name="radial",
    )(
        offsets,
        density,
        weights,
        velocity,
        below.reshape(-1, LANES),
        above.reshape(-1, LANES),
        tables,
        ready,
    )


def legendre_kernel(inv_ref, m_ref, start_ref, trig_ref, out_ref, s_ref, p_ref, z_ref, e_ref, x_ref):
    block = x_ref.shape[1] // 8
    pairs = out_ref.shape[1]
    degrees = block * pl.num_programs(0)
    lat_count = trig_ref.shape[1]
    base = pl.program_id(0) * block
    wide = lat_count // LANES
    order = jnp.broadcast_to(m_ref[...], (8, LANES))
    quantum = LEVEL * math.log(2.0)

    def columns(i):
        return slice(i * LANES, (i + 1) * LANES)

    @pl.when(pl.program_id(0) == 0)
    def _():
        start = jnp.broadcast_to(start_ref[...], (8, LANES))
        for i in range(wide):
            log_value = start + order * trig_ref[1:2, columns(i)]
            level = jnp.minimum(jnp.ceil(log_value * (1.0 / quantum)), 0.0)
            z_ref[:, columns(i)] = (
                jnp.exp(log_value - level * quantum) * trig_ref[2:3, columns(i)]
            )
            e_ref[:, columns(i)] = level
        zero = jnp.zeros((8, lat_count), jnp.float32)
        s_ref[...] = zero
        p_ref[...] = zero

    def eight(chunk, _):
        levels, scales, current, older = [], [], [], []
        for i in range(wide):
            s = s_ref[:, columns(i)]
            p = p_ref[:, columns(i)]
            e = e_ref[:, columns(i)]
            grow = (jnp.maximum(jnp.abs(s), jnp.abs(p)) > 1.0) & (e < 0.0)
            shrink = jnp.where(grow, 2.0**-LEVEL, 1.0)
            e = e + jnp.where(grow, 1.0, 0.0)
            e_ref[:, columns(i)] = e
            current.append(s * shrink)
            older.append(p * shrink)
            scales.append(
                jnp.where(
                    e > -0.5,
                    1.0,
                    jnp.where(e > -1.5, 2.0**-LEVEL, jnp.where(e > -2.5, 2.0 ** (-2 * LEVEL), 0.0)),
                )
            )
        first = base + chunk * 8
        before = jnp.maximum(first - 1, 0)
        before_f = before.astype(jnp.float32)
        back = jnp.maximum((before_f * before_f - order * order) * inv_ref[before], 1e-7)
        back = jnp.sqrt(back)
        for step in range(8):
            degree = first + step
            level = degree.astype(jnp.float32)
            ratio = jnp.maximum((level * level - order * order) * inv_ref[degree], 1e-7)
            up = lax.rsqrt(ratio)
            up_back = up * back
            back = ratio * up
            starting = order == level
            for i in range(wide):
                entry = jnp.where(starting, z_ref[:, columns(i)], 0.0) - up_back * older[i]
                value = (up * trig_ref[0:1, columns(i)]) * current[i] + entry
                older[i] = current[i]
                current[i] = value
                x_ref[i, pl.ds(chunk * 8 + step, 8, stride=block), :] = value * scales[i]
        for i in range(wide):
            s_ref[:, columns(i)] = current[i]
            p_ref[:, columns(i)] = older[i]
        return 0

    lax.fori_loop(0, block // 8, eight, 0)

    def keep(o, row):
        rows = pl.ds(pl.multiple_of(row, block), block)
        for i in range(wide):
            high, low = split(x_ref[i, o * block : (o + 1) * block])
            out_ref[0, o % pairs, rows, columns(i)] = high
            out_ref[1, o % pairs, rows, columns(i)] = low

    for o in range(pairs):
        keep(o, base)

    @pl.when(base * 2 >= degrees)
    def _():
        for o in range(pairs, 2 * pairs):
            keep(o, base + degrees // 2)


def legendre_table(orders, lat_count, degrees):
    colatitude = np.pi * (np.arange(lat_count) + 0.5) / lat_count
    sine = np.sin(colatitude)
    trig = np.stack(
        [np.cos(colatitude), np.log(sine), math.sqrt(np.pi / lat_count) * sine]
    ).astype(np.float32)
    ladder = np.arange(1, degrees)
    logs = 0.5 * math.log(0.5) + np.concatenate(
        [[0.0], np.cumsum(0.5 * np.log((2.0 * ladder + 1.0) / (2.0 * ladder)))]
    )
    level = np.arange(degrees, dtype=np.float64)
    inverse = (1.0 / np.maximum(4.0 * level * level - 1.0, 1.0)).astype(np.float32)
    start = jnp.take(jnp.asarray(logs, jnp.float32), orders)[:, None]
    block = 64
    shape = (2, 4, degrees * 3 // 2, lat_count)
    vmem = pl.BlockSpec(memory_space=pltpu.VMEM)
    return pl.pallas_call(
        legendre_kernel,
        grid=(degrees // block,),
        in_specs=[pl.BlockSpec(memory_space=pltpu.SMEM), vmem, vmem, vmem],
        out_specs=pl.BlockSpec(shape, lambda i: (0, 0, 0, 0)),
        out_shape=jax.ShapeDtypeStruct(shape, jnp.bfloat16),
        scratch_shapes=[pltpu.VMEM((8, lat_count), jnp.float32)] * 4
        + [pltpu.VMEM((lat_count // LANES, 8 * block, LANES), jnp.float32)],
        name="legendre_table",
    )(inverse, orders.astype(jnp.float32)[:, None], start, trig)


def project_kernel(begin, m_ref, o_ref, rad_ref, z_ref, t_ref, e_ref, *refs):
    *out_refs, tile_ref, eig_ref, s_ref, q_ref, sem = refs
    lat_count = tile_ref.shape[-1]
    block = LANES
    shells, modes, degrees = e_ref.shape
    quarter = modes // 4
    pairs = q_ref.shape[1]
    copies = [
        pltpu.make_async_copy(t_ref.at[:, begin + pair], tile_ref.at[pair], sem.at[pair])
        for pair in range(pairs)
    ]
    eigen_copy = pltpu.make_async_copy(e_ref, eig_ref, sem.at[pairs])
    copies[0].start()
    eigen_copy.start()
    for copy in copies[1:]:
        copy.start()
    degree = lax.broadcasted_iota(jnp.int32, (degrees, LANES), 0).astype(jnp.float32)
    factor = degree * (degree + 1.0)

    for pair in range(pairs):
        copies[pair].wait()
        found = []
        for which, (first, count) in enumerate(((0, degrees), (degrees // 2, degrees // 2))):
            o = o_ref[which, begin + pair]
            data = jnp.concatenate(split(z_ref[pl.ds(o, lat_count, stride=8), :]), axis=1)
            rows = slice(which * degrees, which * degrees + count)
            table = jnp.concatenate([tile_ref[pair, 0, rows], tile_ref[pair, 1, rows]], axis=0)
            parts = jnp.dot(table, data, preferred_element_type=jnp.float32)
            both = parts[:count, :LANES] + (parts[:count, LANES:] + parts[count:, :LANES])
            source = both - factor[first : first + count] * pltpu.roll(both, LANES // 2, 1)
            for b in range(count // block):
                s_ref[len(found) + b] = source[b * block : (b + 1) * block].T
            found += [first + b * block for b in range(count // block)]
        if pair == 0:
            eigen_copy.wait()
        kept = []
        for i, first in enumerate(found):
            totals = [jnp.zeros((modes, block), jnp.float32) for _ in range(2)]
            for r in range(shells):
                eigen = eig_ref[r, :, first : first + block]
                for part in range(2):
                    row = part * shells + r
                    totals[part] = totals[part] + eigen * s_ref[i, row : row + 1, :]
            kept.append(totals)
        low_blocks = degrees // block
        wide_pair = m_ref[begin + pair] < block
        places = [
            [jnp.where(wide_pair, x, y) for x, y in zip(kept[0], kept[low_blocks])]
        ] + kept[1:low_blocks] + kept[low_blocks + 1 :]
        for place, totals in enumerate(places):
            for part in range(2):
                for q in range(4):
                    q_ref[q, pair, place, part] = totals[part][q * quarter : (q + 1) * quarter]

    for relative, out_ref in enumerate(out_refs):
        out_ref[...] = q_ref[rad_ref[0] ^ relative]


def projected(begin, pairs, lower, places, rad, spectrum, table, eigen):
    lat_count = table.shape[-1]
    shells, modes, degrees = eigen.shape
    block = LANES
    smem = pl.BlockSpec(memory_space=pltpu.SMEM)
    vmem = pl.BlockSpec(memory_space=pltpu.VMEM)
    hbm = pl.BlockSpec(memory_space=pl.ANY)
    shape = (pairs, degrees // block + 1, 2, modes // 4, block)
    return pl.pallas_call(
        functools.partial(project_kernel, begin),
        in_specs=[smem, smem, smem, vmem, hbm, hbm],
        out_specs=[vmem] * 4,
        out_shape=[jax.ShapeDtypeStruct(shape, jnp.float32)] * 4,
        scratch_shapes=[
            pltpu.VMEM((pairs, 2) + table.shape[2:], jnp.bfloat16),
            pltpu.VMEM(eigen.shape, jnp.float32),
            pltpu.VMEM((degrees * 3 // 2 // block, LANES, block), jnp.float32),
            pltpu.VMEM((4,) + shape, jnp.float32),
            pltpu.SemaphoreType.DMA((pairs + 1,)),
        ],
        name="project",
    )(lower, places, rad, spectrum.reshape(lat_count * 8, LANES), table, eigen)


def finish_kernel(m_ref, slot_ref, *refs):
    *in_refs, out_ref = refs
    groups = len(in_refs) // 4
    pairs, places = in_refs[0].shape[:2]
    block = in_refs[0].shape[-1]
    for group in range(groups):
        mine = in_refs[group * 4 : group * 4 + 4]
        for pair in range(pairs):
            at = group * pairs + pair
            wide_pair = m_ref[at] < block
            low, high = slot_ref[0, at], slot_ref[1, at]

            def total(place):
                return (mine[0][pair, place] + mine[1][pair, place]) + (
                    mine[2][pair, place] + mine[3][pair, place]
                )

            first = total(0)
            zero = jnp.zeros_like(first)
            out_ref[low, :, :, 0:block] = jnp.where(wide_pair, first, zero)
            for place in range(1, places - 1):
                out_ref[low, :, :, place * block : (place + 1) * block] = total(place)
            for place in range(places - 3):
                out_ref[high, :, :, place * block : (place + 1) * block] = zero
            out_ref[high, :, :, (places - 3) * block : (places - 2) * block] = jnp.where(
                wide_pair, zero, first
            )
            out_ref[high, :, :, (places - 2) * block :] = total(places - 1)


def finished(lower, slots, parts):
    pairs, places, kinds, modes, block = parts[0].shape
    count = 2 * pairs * (len(parts) // 4)
    smem = pl.BlockSpec(memory_space=pltpu.SMEM)
    vmem = pl.BlockSpec(memory_space=pltpu.VMEM)
    return pl.pallas_call(
        finish_kernel,
        in_specs=[smem, smem] + [vmem] * len(parts),
        out_specs=vmem,
        out_shape=jax.ShapeDtypeStruct((count, kinds, modes, (places - 1) * block), jnp.float32),
        name="finish",
    )(lower, slots, *parts)


def body(velocity, density, offsets, radial_weights, angular_scale, order_table, eigenfunctions):
    lats, lon = velocity.shape[2:]
    velocity = jnp.transpose(velocity, (0, 2, 1, 3))
    degrees = order_table.shape[0]
    groups = lax.axis_size("lat")
    size = lax.axis_size("rad")
    lat_count = lats * groups
    where = lax.axis_index("lat")

    top, bottom = halo_cross(density, velocity)
    up = [(i, i + 1) for i in range(size - 1)]
    below = lax.ppermute(top, "rad", up)
    above = lax.ppermute(bottom, "rad", [(j, i) for i, j in up])
    pairs = order_table.reshape(degrees // 2, 2)
    tables = gathered_tables(pairs[:, 0][None, :], master_tables(lon, degrees))
    by_slot = fourier(
        offsets, density, radial_weights, angular_scale, velocity, below, above, tables
    )
    by_slot = by_slot.reshape(groups, lats, 8, LANES)
    gathered = lax.all_to_all(by_slot, "lat", split_axis=0, concat_axis=0, tiled=True)
    gathered = gathered.reshape(lat_count, 8, LANES)

    first = lax.dynamic_slice_in_dim(pairs, where * 4, 4)[:, 0]
    second = degrees - 1 - first
    first_half = (first & 1) == (where & 1)
    eigen = jnp.transpose(eigenfunctions, (2, 1, 0))
    first_low = first < degrees // 2
    lower = jnp.where(first_low, first, second)
    orders = jnp.concatenate([lower, degrees - 1 - lower])
    table = legendre_table(orders, lat_count, degrees)
    number = jnp.arange(4, dtype=jnp.int32)
    slot = 2 * number + jnp.where(first_low, 0, 1)
    slots = jnp.stack([slot, slot ^ 1])
    row = number + jnp.where(first_low == first_half, 0, 4)
    places = jnp.stack([row, row ^ 4])
    rad = lax.axis_index("rad")[None]
    parts = []
    for begin in (0, 2):
        own, *others = projected(
            begin, 2, lower, places, rad, gathered, table, eigen
        )
        parts.append(own)
        for relative, other in enumerate(others, 1):
            swap = [(i, i ^ relative) for i in range(size)]
            parts.append(lax.ppermute(other, "rad", swap))
    return finished(lower, slots, parts)


def solution(mesh):
    placed = (
        P(None, "rad", "lat", None),
        P("rad"),
        P(),
        P(None, None, "rad"),
        P("rad"),
        P(),
        P(None, None, "rad"),
    )
    return jax.shard_map(
        body, mesh=mesh, in_specs=placed, out_specs=P("lat", None, "rad", None), check_vma=False
    )
```

time: 177 us -> 153 us (0.86)
  blocking collectives: 18.5 us -> 0 us
  Pallas kernels: 49 us -> 65.7 us
  local copies, waits for them, and re-layouts: 23.8 us -> 8.91 us
  waiting for transfers between devices: 54.4 us -> 46.4 us
  starting transfers between devices: 19.9 us -> 27.4 us
  other arithmetic: 8.22 us -> 3.19 us
    all_to_all x1 -> x0, blocking collectives: 18.5 us -> none  [body(): lax.all_to_all(partial, 'rad', split_axis=0, concat_axis=0, tiled=True)]
    all_to_all x1, waiting for transfers between devices: 54.4 us -> 41.5 us  [body(): lax.all_to_all(by_slot, 'lat', split_axis=0, concat_axis=0, tiled=True)]
    pallas_call x1, Pallas kernels: 9.17 us -> 21.7 us  [legendre_table(): pl.pallas_call(legendre_kernel, grid=(degrees // block,), in_specs=[pl.Bl...]
    ppermute x2 -> x8, starting transfers between devices: 7.93 us -> 15.6 us  [the longest x6 7.63 us: body(): parts.append(lax.ppermute(other, 'rad', swap))]
    ppermute x2 -> x8, waiting for transfers between devices: 0.01 us -> 4.83 us  [the longest x6 4.83 us: body(): parts.append(lax.ppermute(other, 'rad', swap))]
    pallas_call x3 -> x7, Pallas kernels: 39.8 us -> 44 us  [the longest x2 16.1 us: projected(): pl.pallas_call(functools.partial(project_kernel, begin), in_specs=[smem,...]
    ppermute x2 -> x0, local copies, waits for them, and re-layouts: 3.95 us -> none  [the longest x1 1.98 us: body(): lax.ppermute(cross((velocity[:, :HALO], density[:HALO])), 'rad', down)]
    slice x4 -> x1, local copies, waits for them, and re-layouts: 3.93 us -> 0.68 us  [body(): tables = gathered_tables(pairs[:, 0][None, :], master_tables(lon, degrees))]
  transfers between devices with their start and end apart: 3 -> 9, of which waited for: 1 -> 4; matrix products, arithmetic and copies ran while one was open for 13% -> 6% of each run, Pallas kernels for 9% -> 27%
where the time goes in v2:
time: 153 us; the launch traced here: 152 us
  Pallas kernels  65.7 us (43%)
  waiting for transfers between devices  46.4 us (30%)
  starting transfers between devices  27.4 us (18%)
  local copies, waits for them, and re-layouts  8.91 us (6%)
  other arithmetic  3.19 us (2%)
    all_to_all x1, waiting for transfers between devices, body(): lax.all_to_all(by_slot, 'lat', split_axis=0, concat_axis=0, tiled=True)  41.5 us
    pallas_call x1, Pallas kernels, legendre_table(): pl.pallas_call(legendre_kernel, grid=(degrees // block,), in_specs=[pl.Bl...  21.7 us
    pallas_call x2, Pallas kernels, projected(): pl.pallas_call(functools.partial(project_kernel, begin), in_specs=[smem,...  16.1 us
    all_to_all x1, starting transfers between devices, body(): lax.all_to_all(by_slot, 'lat', split_axis=0, concat_axis=0, tiled=True)  11.9 us
    pallas_call x1, Pallas kernels, fourier(): pl.pallas_call(radial_kernel, in_specs=[smem] * 3 + [hbm] + [vmem] * 4, o...  10.6 us
    pallas_call x1, Pallas kernels, fourier(): pl.pallas_call(angular_kernel, in_specs=[smem, smem, hbm, vmem], out_spec...  7.96 us
    ppermute x6, starting transfers between devices, body(): parts.append(lax.ppermute(other, 'rad', swap))  7.63 us
    unnamed x27, local copies, waits for them, and re-layouts  7.36 us
  transfers between devices with their start and end apart: 9, of which 4 were waited for; matrix products, arithmetic and copies ran while one was open for 6% of the time, Pallas kernels for 27%

profile of v2, /device:TPU:1, one launch (start us, length us, event | category | flops | bytes accessed | tf_op | source)
XLA Modules:
  0.0 151.8 jit_solution(6932444159708250105)
XLA Ops:
  0.0 3.5 %halo_cross.1 = (f32[2,3,144,128]{3,2,1,0:T(8,128)}, f32[2,3,144,128]{3,2,1,0:T(8,128)}) custom-call(f32[32]{0:T(128)} %rho_ref.5, bf16[3,12,32,1536]{3,2,1,0:T(8,128)(2,1)} %bitcast.19), custom_call_target="tpu_custom_call" | custom-call | tf_op jit(solution)/shard_map/halo_cross/pallas_call | solution.py:99
  3.5 6.0 %collective-permute-start = (f32[2,3,144,128]{3,2,1,0:T(8,128)}, f32[2,3,144,128]{3,2,1,0:T(8,128)S(1)}, u32[]{:S(2)}, u32[]{:S(2)}) collective-permute-start(f32[2,3,144,128]{3,2,1,0:T(8,128)} %get-tuple-element.15), channel_id=1, source_target_pairs={{0,64},{64,128},{128,192},{1,65},{65,129},{129,193},{2,66},{66,130... | collective-permute-start | bytes 1327112 | tf_op jit(solution)/shard_map/ppermute | solution.py:585
  9.5 1.9 %collective-permute-start.1 = (f32[2,3,144,128]{3,2,1,0:T(8,128)}, f32[2,3,144,128]{3,2,1,0:T(8,128)S(1)}, u32[]{:S(2)}, u32[]{:S(2)}) collective-permute-start(f32[2,3,144,128]{3,2,1,0:T(8,128)} %get-tuple-element.16), channel_id=1, source_target_pairs={{64,0},{128,64},{192,128},{65,1},{129,65},{193,129},{66,2},{130,66... | collective-permute-start | bytes 1327112 | tf_op jit(solution)/shard_map/ppermute | solution.py:586
  11.5 0.0 copy-done.10
  11.5 0.1 reshape.250
  11.6 0.7 slice_reduce_fusion
  12.3 4.0 %gather_rows.1.t_ref = bf16[2,4,256,768]{3,2,1,0:T(8,128)(2,1)} custom-call(s32[1,256]{1,0:T(1,128)} %bitcast.29, bf16[2,4,256,768]{3,2,1,0:T(8,128)(2,1)} %constant.46.clone.table_ref), custom_call_target="tpu_custom_call" | custom-call | tf_op jit(solution)/shard_map/gather_rows/pallas_call | solution.py:52
  16.3 8.0 %angular.1.a_ref = f32[32,2,6,8,128]{4,3,2,1,0:T(8,128)} custom-call(f32[32]{0:T(128)} %rho_ref.5, f32[32]{0:T(128)} %ang_ref.1, bf16[3,12,32,1536]{3,2,1,0:T(8,128)(2,1)} %bitcast.20, bf16[2,4,256,768]{3,2,1,0:T(8,128)(2,1)} %gather_rows.1.t_ref), custom_call_target="tpu_custom_call" | custom-call | tf_op jit(solution)/shard_map/angular/pallas_call | solution.py:299
  24.2 0.0 collective-permute-done
  24.2 0.0 copy-start.2
  24.2 0.0 collective-permute-done.1
  24.3 0.0 copy-start.3
  24.3 0.7 copy-done.2
  25.0 0.2 copy-done.3
  25.2 10.6 %radial.1 = f32[32,2,12,8,128]{4,3,2,1,0:T(8,128)} custom-call(s32[4]{0:T(128)} %off_ref.1, f32[32]{0:T(128)} %rho_ref.5, f32[2,4,32]{2,1,0:T(4,128)} %w_ref.1, bf16[3,12,32,1536]{3,2,1,0:T(8,128)(2,1)} %bitcast.21, f32[864,128]{1,0:T(8,128)} %bitcast.27, f32[864,128]{1,0:T(8,128)} %bitcast.28, bf16[2,4,256,768]{3,2,1,0:T(8,128)(2,1)} %gather_rows.1.t_ref, ...), custom_call_target="tpu_custom_call" | custom-call | tf_op jit(solution)/shard_map/radial/pallas_call | solution.py:307
  35.8 0.0 copy-start
  35.8 11.9 %all-to-all-start = ((f32[64,12,8,128]{3,2,1,0:T(8,128)}), f32[64,12,8,128]{3,2,1,0:T(8,128)S(1)}, u32[]{:S(2)}, u32[]{:S(2)}) async-start(f32[64,12,8,128]{3,2,1,0:T(8,128)} %bitcast.26), calls=%async_computation | async-start | bytes 6291456 | tf_op jit(solution)/shard_map/all_to_all | solution.py:593
  47.7 0.7 fusion.1
  48.4 0.6 gather_fusion
  49.1 0.1 copy.24
  49.1 4.2 %copy.27 = f32[512,32,32]{0,1,2:T(8,128)} copy(f32[512,32,32]{0,2,1:T(8,128)} %param.17) | data formatting | bytes 4194304 | tf_op args[6]
  53.3 0.6 and_select_fusion.start_ref
  53.9 21.7 %legendre_table.1.t_ref = bf16[2,4,768,768]{3,2,1,0:T(8,128)(2,1)} custom-call(f32[512]{0:T(512)} %constant.48.clone.inv_ref, f32[8,1]{1,0:T(8,128)} %get-tuple-element.32.m_ref, f32[8,1]{1,0:T(8,128)} %and_select_fusion.start_ref, f32[3,768]{1,0:T(4,128)} %constant.49.clone.trig_ref), custom_call_target="tpu_custom_call" | custom-call | tf_op jit(solution)/shard_map/legendre_table/pallas_call | solution.py:436
  75.6 0.1 select_reduce_fusion
  75.7 0.6 pad_add_fusion.2.o_ref
  76.3 0.5 compare_select_fusion.1.m_ref
  76.9 41.5 %all-to-all-done = f32[64,12,8,128]{3,2,1,0:T(8,128)S(1)} async-done(((f32[64,12,8,128]{3,2,1,0:T(8,128)}), f32[64,12,8,128]{3,2,1,0:T(8,128)S(1)}, u32[]{:S(2)}, u32[]{:S(2)}) %all-to-all-start) | async-done | bytes 3145760 | tf_op jit(solution)/shard_map/all_to_all | solution.py:593
  118.4 1.6 %copy-done.1 = f32[64,12,8,128]{3,2,1,0:T(8,128)} copy-done((f32[64,12,8,128]{3,2,1,0:T(8,128)}, f32[64,12,8,128]{3,2,1,0:T(8,128)S(1)}, u32[]{:S(2)}) %copy-start.1) | copy-done | bytes 3145752
  120.1 8.0 %project.2 = (f32[2,5,2,8,128]{4,3,2,1,0:T(8,128)}, f32[2,5,2,8,128]{4,3,2,1,0:T(8,128)}, f32[2,5,2,8,128]{4,3,2,1,0:T(8,128)}, f32[2,5,2,8,128]{4,3,2,1,0:T(8,128)}) custom-call(s32[4]{0:T(128)} %compare_select_fusion.1.m_ref, s32[2,4]{1,0:T(2,128)} %pad_add_fusion.2.o_ref, s32[1]{0:T(128)} %bitcast.rad_ref, f32[6144,128]{1,0:T(8,128)} %bitcast.22, ...), custom_call_target="tpu_custom_call" | custom-call | tf_op jit(solution)/shard_map/project/pallas_call | solution.py:514
  128.1 0.3 collective-permute-start.2
  128.4 8.1 %project.3 = (f32[2,5,2,8,128]{4,3,2,1,0:T(8,128)}, f32[2,5,2,8,128]{4,3,2,1,0:T(8,128)}, f32[2,5,2,8,128]{4,3,2,1,0:T(8,128)}, f32[2,5,2,8,128]{4,3,2,1,0:T(8,128)}) custom-call(s32[4]{0:T(128)} %compare_select_fusion.1.m_ref, s32[2,4]{1,0:T(2,128)} %pad_add_fusion.2.o_ref, s32[1]{0:T(128)} %bitcast.rad_ref, f32[6144,128]{1,0:T(8,128)} %bitcast.23, ...), custom_call_target="tpu_custom_call" | custom-call | tf_op jit(solution)/shard_map/project/pallas_call | solution.py:514
  136.5 2.9 %collective-permute-start.3 = (f32[2,5,2,8,128]{4,3,2,1,0:T(8,128)S(1)}, f32[2,5,2,8,128]{4,3,2,1,0:T(8,128)S(1)}, u32[]{:S(2)}, u32[]{:S(2)}) collective-permute-start(f32[2,5,2,8,128]{4,3,2,1,0:T(8,128)S(1)} %copy-done.12), channel_id=1, source_target_pairs={{0,128},{64,192},{128,0},{192,64},{1,129},{65,193},{129,1},{193,65... | collective-permute-start | bytes 245768 | tf_op jit(solution)/shard_map/ppermute | solution.py:618
  139.3 0.8 collective-permute-start.4
  140.2 0.0 collective-permute-start.5
  140.2 2.5 %collective-permute-start.6 = (f32[2,5,2,8,128]{4,3,2,1,0:T(8,128)}, f32[2,5,2,8,128]{4,3,2,1,0:T(8,128)S(1)}, u32[]{:S(2)}, u32[]{:S(2)}) collective-permute-start(f32[2,5,2,8,128]{4,3,2,1,0:T(8,128)} %get-tuple-element.23), channel_id=1, source_target_pairs={{0,128},{64,192},{128,0},{192,64},{1,129},{65,193},{129,1},{193,65... | collective-permute-start | bytes 245768 | tf_op jit(solution)/shard_map/ppermute | solution.py:618
  142.7 0.0 collective-permute-done.2.refs_1_
  142.7 1.1 collective-permute-start.7
  143.8 0.6 pad_add_fusion.1.slot_ref
  144.4 0.0 collective-permute-done.3.refs_2_
  144.4 1.2 collective-permute-done.4.refs_3_
  145.6 0.0 collective-permute-done.5.refs_5_
  145.6 1.3 collective-permute-done.6.refs_6_
  146.9 2.4 %collective-permute-done.7.refs_7_ = f32[2,5,2,8,128]{4,3,2,1,0:T(8,128)S(1)} collective-permute-done((f32[2,5,2,8,128]{4,3,2,1,0:T(8,128)}, f32[2,5,2,8,128]{4,3,2,1,0:T(8,128)S(1)}, u32[]{:S(2)}, u32[]{:S(2)}) %collective-permute-start.7) | collective-permute-done | bytes 81952 | tf_op jit(solution)/shard_map/ppermute | solution.py:618
  149.2 0.0 copy-done.5
  149.3 0.0 copy-done.7
  149.3 0.0 copy-done.8
  149.3 0.6 copy-done.9
  149.9 1.9 %finish.1 = f32[8,2,8,512]{3,2,1,0:T(8,128)} custom-call(s32[4]{0:T(128)} %compare_select_fusion.1.m_ref, s32[2,4]{1,0:T(2,128)} %pad_add_fusion.1.slot_ref, f32[2,5,2,8,128]{4,3,2,1,0:T(8,128)} %get-tuple-element.17.refs_0_, f32[2,5,2,8,128]{4,3,2,1,0:T(8,128)} %copy-done.4, f32[2,5,2,8,128]{4,3,2,1,0:T(8,128)} %copy-done.5, ...), custom_call_target="tpu_custom_call" | custom-call | tf_op jit(solution)/shard_map/finish/pallas_call | solution.py:565
  (19 shorter events, 0.1 us)
Async XLA Ops:
  0.0 11.5 %copy-start.10 = (s32[512]{0:T(512)S(1)}, s32[512]{0:T(512)}, u32[]{:S(2)}) copy-start(s32[512]{0:T(512)} %param.16) | copy-start | bytes 6148
  3.5 20.7 %collective-permute-start = (f32[2,3,144,128]{3,2,1,0:T(8,128)}, f32[2,3,144,128]{3,2,1,0:T(8,128)S(1)}, u32[]{:S(2)}, u32[]{:S(2)}) collective-permute-start(f32[2,3,144,128]{3,2,1,0:T(8,128)} %get-tuple-element.15), channel_id=1, source_target_pairs={{0,64},{64,128},{128,192},{1,65},{65,129},{129,193},{2,66},{66,130... | collective-permute-start | bytes 1327112 | tf_op jit(solution)/shard_map/ppermute | solution.py:585
  9.5 14.7 %collective-permute-start.1 = (f32[2,3,144,128]{3,2,1,0:T(8,128)}, f32[2,3,144,128]{3,2,1,0:T(8,128)S(1)}, u32[]{:S(2)}, u32[]{:S(2)}) collective-permute-start(f32[2,3,144,128]{3,2,1,0:T(8,128)} %get-tuple-element.16), channel_id=1, source_target_pairs={{64,0},{128,64},{192,128},{65,1},{129,65},{193,129},{66,2},{130,66... | collective-permute-start | bytes 1327112 | tf_op jit(solution)/shard_map/ppermute | solution.py:586
  24.2 0.8 copy-start.2
  24.3 0.9 copy-start.3
  35.8 12.7 %copy-start = (f32[512]{0:T(512)S(1)}, f32[512]{0:T(512)}, u32[]{:S(2)}) copy-start(f32[512]{0:T(512)} %constant.47.clone) | copy-start | bytes 6148
  35.8 82.6 %all-to-all-start = ((f32[64,12,8,128]{3,2,1,0:T(8,128)}), f32[64,12,8,128]{3,2,1,0:T(8,128)S(1)}, u32[]{:S(2)}, u32[]{:S(2)}) async-start(f32[64,12,8,128]{3,2,1,0:T(8,128)} %bitcast.26), calls=%async_computation | async-start | bytes 6291456 | tf_op jit(solution)/shard_map/all_to_all | solution.py:593
  118.4 1.6 %copy-start.1 = (f32[64,12,8,128]{3,2,1,0:T(8,128)}, f32[64,12,8,128]{3,2,1,0:T(8,128)S(1)}, u32[]{:S(2)}) copy-start(f32[64,12,8,128]{3,2,1,0:T(8,128)S(1)} %all-to-all-done) | copy-start | bytes 9437188
  128.1 8.4 %copy-start.12 = (f32[2,5,2,8,128]{4,3,2,1,0:T(8,128)S(1)}, f32[2,5,2,8,128]{4,3,2,1,0:T(8,128)}, u32[]{:S(2)}) copy-start(f32[2,5,2,8,128]{4,3,2,1,0:T(8,128)} %get-tuple-element.19) | copy-start | bytes 245764
  128.1 11.2 %copy-start.11 = (f32[2,5,2,8,128]{4,3,2,1,0:T(8,128)S(1)}, f32[2,5,2,8,128]{4,3,2,1,0:T(8,128)}, u32[]{:S(2)}) copy-start(f32[2,5,2,8,128]{4,3,2,1,0:T(8,128)} %get-tuple-element.20) | copy-start | bytes 245764
  128.1 14.6 %collective-permute-start.2 = (f32[2,5,2,8,128]{4,3,2,1,0:T(8,128)}, f32[2,5,2,8,128]{4,3,2,1,0:T(8,128)S(1)}, u32[]{:S(2)}, u32[]{:S(2)}) collective-permute-start(f32[2,5,2,8,128]{4,3,2,1,0:T(8,128)} %get-tuple-element.18), channel_id=1, source_target_pairs={{0,64},{64,0},{128,192},{192,128},{1,65},{65,1},{129,193},{193,129... | collective-permute-start | bytes 245768 | tf_op jit(solution)/shard_map/ppermute | solution.py:618
  136.5 7.9 %collective-permute-start.3 = (f32[2,5,2,8,128]{4,3,2,1,0:T(8,128)S(1)}, f32[2,5,2,8,128]{4,3,2,1,0:T(8,128)S(1)}, u32[]{:S(2)}, u32[]{:S(2)}) collective-permute-start(f32[2,5,2,8,128]{4,3,2,1,0:T(8,128)S(1)} %copy-done.12), channel_id=1, source_target_pairs={{0,128},{64,192},{128,0},{192,64},{1,129},{65,193},{129,1},{193,65... | collective-permute-start | bytes 245768 | tf_op jit(solution)/shard_map/ppermute | solution.py:618
  139.3 6.2 %collective-permute-start.4 = (f32[2,5,2,8,128]{4,3,2,1,0:T(8,128)S(1)}, f32[2,5,2,8,128]{4,3,2,1,0:T(8,128)S(1)}, u32[]{:S(2)}, u32[]{:S(2)}) collective-permute-start(f32[2,5,2,8,128]{4,3,2,1,0:T(8,128)S(1)} %copy-done.11), channel_id=1, source_target_pairs={{0,192},{64,128},{128,64},{192,0},{1,193},{65,129},{129,65},{193,1... | collective-permute-start | bytes 245768 | tf_op jit(solution)/shard_map/ppermute | solution.py:618
  140.2 5.4 %collective-permute-start.5 = (f32[2,5,2,8,128]{4,3,2,1,0:T(8,128)}, f32[2,5,2,8,128]{4,3,2,1,0:T(8,128)S(1)}, u32[]{:S(2)}, u32[]{:S(2)}) collective-permute-start(f32[2,5,2,8,128]{4,3,2,1,0:T(8,128)} %get-tuple-element.22), channel_id=1, source_target_pairs={{0,64},{64,0},{128,192},{192,128},{1,65},{65,1},{129,193},{193,129... | collective-permute-start | bytes 245768 | tf_op jit(solution)/shard_map/ppermute | solution.py:618
  140.2 6.7 %collective-permute-start.6 = (f32[2,5,2,8,128]{4,3,2,1,0:T(8,128)}, f32[2,5,2,8,128]{4,3,2,1,0:T(8,128)S(1)}, u32[]{:S(2)}, u32[]{:S(2)}) collective-permute-start(f32[2,5,2,8,128]{4,3,2,1,0:T(8,128)} %get-tuple-element.23), channel_id=1, source_target_pairs={{0,128},{64,192},{128,0},{192,64},{1,129},{65,193},{129,1},{193,65... | collective-permute-start | bytes 245768 | tf_op jit(solution)/shard_map/ppermute | solution.py:618
  142.7 6.5 %copy-start.4 = (f32[2,5,2,8,128]{4,3,2,1,0:T(8,128)}, f32[2,5,2,8,128]{4,3,2,1,0:T(8,128)S(1)}, u32[]{:S(2)}) copy-start(f32[2,5,2,8,128]{4,3,2,1,0:T(8,128)S(1)} %collective-permute-done.2.refs_1_) | copy-start | bytes 245764
  142.7 6.5 %collective-permute-start.7 = (f32[2,5,2,8,128]{4,3,2,1,0:T(8,128)}, f32[2,5,2,8,128]{4,3,2,1,0:T(8,128)S(1)}, u32[]{:S(2)}, u32[]{:S(2)}) collective-permute-start(f32[2,5,2,8,128]{4,3,2,1,0:T(8,128)} %get-tuple-element.24), channel_id=1, source_target_pairs={{0,192},{64,128},{128,64},{192,0},{1,193},{65,129},{129,65},{193,1... | collective-permute-start | bytes 245768 | tf_op jit(solution)/shard_map/ppermute | solution.py:618
  144.4 4.8 %copy-start.5 = (f32[2,5,2,8,128]{4,3,2,1,0:T(8,128)}, f32[2,5,2,8,128]{4,3,2,1,0:T(8,128)S(1)}, u32[]{:S(2)}) copy-start(f32[2,5,2,8,128]{4,3,2,1,0:T(8,128)S(1)} %collective-permute-done.3.refs_2_) | copy-start | bytes 245764
  145.6 3.7 %copy-start.6 = (f32[2,5,2,8,128]{4,3,2,1,0:T(8,128)}, f32[2,5,2,8,128]{4,3,2,1,0:T(8,128)S(1)}, u32[]{:S(2)}) copy-start(f32[2,5,2,8,128]{4,3,2,1,0:T(8,128)S(1)} %collective-permute-done.4.refs_3_) | copy-start | bytes 245764
  145.6 3.7 %copy-start.7 = (f32[2,5,2,8,128]{4,3,2,1,0:T(8,128)}, f32[2,5,2,8,128]{4,3,2,1,0:T(8,128)S(1)}, u32[]{:S(2)}) copy-start(f32[2,5,2,8,128]{4,3,2,1,0:T(8,128)S(1)} %collective-permute-done.5.refs_5_) | copy-start | bytes 245764
  146.9 2.4 %copy-start.8 = (f32[2,5,2,8,128]{4,3,2,1,0:T(8,128)}, f32[2,5,2,8,128]{4,3,2,1,0:T(8,128)S(1)}, u32[]{:S(2)}) copy-start(f32[2,5,2,8,128]{4,3,2,1,0:T(8,128)S(1)} %collective-permute-done.6.refs_6_) | copy-start | bytes 245764
  149.2 0.6 copy-start.9
